TPU v7x, 256 devices: a whole 4x4x8 slice. The times are simulated.
256 devices in a mesh: det: 64 (over z, y, core), tm: 4 (over x).
Axes of the slice: x: 4, y: 4, z: 8, core: 2. Of those that a mesh axis runs over, the one named last changes fastest.
Arguments:
- time_streams: float32 [64, 1, 4096], P('det', None, 'tm'), may hold values from -12 to 12
- pol_angle: float32 [64, 1, 4096], P('det', None, 'tm'), may hold values from -3.140625 to 3.140625
- offsets: int32 [64, 1, 4096], P('det', None, 'tm'), may hold values from 0 to 255
- block_slots: int32 [64, 1, 16], P('det', None, 'tm'), may hold values from 0 to 127
- hit_ids: int32 [64, 128], P('det'), may hold values from 0 to 1023, as said below
- valid_counts: int32 [64, 1], P('det'), may hold values from 1024 to 4096
- filter_taps: float32 [64, 1, 65], P('det'), may hold values from -0.75 to 0.75
- white_weight: float32 [64, 1], P('det'), may hold values from 0.5 to 2
Outputs:
- solution_map: float32 [1024, 3, 256], P('det')
- precond_residual: float32 [1024, 3, 256], P('det')
Inputs may be any that keep to these rules, and one draw needn't show every extreme that they name: `hit_ids`: slot o * 2 + c of a section names a block of o * 16 .. (o + 1) * 16 - 1, and the 2 blocks of one o in one section differ.
All inputs are finite; a program needn't handle non-finite values.
Results may differ from a plain program's by a relative error of at most 0.0003.
Values sent between devices are 32-bit elements; how exact they have to be, the bound alone decides.
A program may use at most 128 MiB of HBM per device.

v0:
```python
import jax
import jax.numpy as jnp
from jax import lax
from jax.sharding import PartitionSpec as P

BLK = 256
WIN = 256
BAND = 64
ITERS = 2
NDET = 1
TCH = 1024
BPD = 16
CAP = 2


highest = lax.Precision.HIGHEST


def with_halo(cells, sides, width):
    for axis, dim in sides:
        count = lax.axis_size(axis)
        ends = count - 1
        head = lax.slice_in_dim(cells, 0, width, axis=dim)
        tail = lax.slice_in_dim(cells, cells.shape[dim] - width, cells.shape[dim], axis=dim)
        cells = jnp.concatenate(
            [
                lax.ppermute(tail, axis, [(i, (i + 1) % count) for i in range(ends)]),
                cells,
                lax.ppermute(head, axis, [((i + 1) % count, i) for i in range(ends)]),
            ],
            axis=dim,
        )
    return cells


def lag_table(filter_taps, white_weight):
    columns = []
    for shift_lag in range(BAND + 1):
        columns.append(
            jnp.sum(
                filter_taps[..., : BAND + 1 - shift_lag] * filter_taps[..., shift_lag:], axis=-1
            )
        )
    lags = jnp.stack(columns, axis=-1)
    return lags.at[..., 0].add(white_weight)


def toeplitz_matrix(lags):
    row_index = jnp.arange(WIN + 2 * BAND, dtype=jnp.int32)[:, None]
    col_index = jnp.arange(WIN, dtype=jnp.int32)[None, :]
    distance = jnp.abs(row_index - BAND - col_index)
    inside = distance <= BAND
    clipped = jnp.minimum(distance, BAND)
    return jnp.where(inside[None], lags[:, clipped], 0.0)


def precondition(weights, residual):
    entry_aa = 1.0 + weights[:, 0]
    entry_ab = weights[:, 1]
    entry_ac = weights[:, 2]
    entry_bb = 1.0 + weights[:, 3]
    entry_bc = weights[:, 4]
    entry_cc = 1.0 + weights[:, 5]
    minor_aa = entry_bb * entry_cc - entry_bc * entry_bc
    minor_ab = entry_ac * entry_bc - entry_ab * entry_cc
    minor_ac = entry_ab * entry_bc - entry_ac * entry_bb
    minor_bb = entry_aa * entry_cc - entry_ac * entry_ac
    minor_bc = entry_ab * entry_ac - entry_aa * entry_bc
    minor_cc = entry_aa * entry_bb - entry_ab * entry_ab
    determinant = entry_aa * minor_aa + entry_ab * minor_ab + entry_ac * minor_ac
    stokes_i = residual[:, 0]
    stokes_q = residual[:, 1]
    stokes_u = residual[:, 2]
    return jnp.stack(
        [
            (minor_aa * stokes_i + minor_ab * stokes_q + minor_ac * stokes_u) / determinant,
            (minor_ab * stokes_i + minor_bb * stokes_q + minor_bc * stokes_u) / determinant,
            (minor_ac * stokes_i + minor_bc * stokes_q + minor_cc * stokes_u) / determinant,
        ],
        axis=1,
    )


def global_dot(left, right):
    return lax.psum(jnp.sum(left * right), "det")


def per_device(
    time_streams, pol_angle, offsets, block_slots, hit_ids, valid_counts, filter_taps, white_weight
):
    det_count = lax.axis_size("det")
    block_count = TCH // WIN
    lags = lag_table(filter_taps[0], white_weight[0])
    matrix = toeplitz_matrix(lags)
    hit_row = hit_ids[0]
    hit_total = hit_row.shape[0]
    span_start = lax.axis_index("tm") * TCH
    sample_time = span_start + jnp.arange(TCH, dtype=jnp.int32)
    live_mask = (
        (sample_time[None, :] < valid_counts[0][:, None])
        .astype(jnp.float32)
        .reshape(NDET, block_count, WIN)
    )
    cosine = jnp.cos(2.0 * pol_angle[0]).reshape(NDET, block_count, WIN)
    sine_term = jnp.sin(2.0 * pol_angle[0]).reshape(NDET, block_count, WIN)
    pixel_pick = (
        offsets[0].reshape(NDET, block_count, WIN, 1) == jnp.arange(BLK, dtype=jnp.int32)
    ).astype(jnp.float32)
    slot_pick = (jnp.arange(hit_total, dtype=jnp.int32)[:, None] == block_slots[0]).astype(
        jnp.float32
    )
    place_pick = (
        (hit_row.reshape(det_count, CAP) % BPD)[:, :, None] == jnp.arange(BPD, dtype=jnp.int32)
    ).astype(jnp.float32)

    def noise_filter(signal):
        padded = with_halo(signal.reshape(NDET, TCH), (("tm", 1),), BAND)
        extended = jnp.pad(padded, ((0, 0), (0, WIN - 2 * BAND)))
        leading = extended[:, :TCH].reshape(NDET, block_count, WIN)
        trailing = extended[:, WIN : WIN + TCH].reshape(NDET, block_count, WIN)[:, :, : 2 * BAND]
        window = jnp.concatenate([leading, trailing], axis=2)
        return jnp.einsum("djo,dok->djk", window, matrix, precision=highest)

    def bin_samples(components):
        comp_count = components.shape[2]
        per_block = jnp.einsum("djwp,djkw->djkp", pixel_pick, components, precision=highest)
        summed = jnp.dot(
            slot_pick, per_block.reshape(NDET * block_count, comp_count * BLK), precision=highest
        )
        return summed.reshape(hit_total, comp_count, BLK)

    def to_owner_blocks(binned):
        comp_count = binned.shape[1]
        pixel_part = binned.shape[2]
        grouped = binned.reshape(det_count, CAP, comp_count * pixel_part)
        whole_map = jnp.einsum("ocb,ocx->obx", place_pick, grouped, precision=highest)
        whole_map = whole_map.reshape(det_count * BPD, comp_count, pixel_part)
        owned_map = lax.psum_scatter(whole_map, "det", scatter_dimension=0, tiled=True)
        owned_map = lax.psum(owned_map, "tm")
        return owned_map

    filtered = noise_filter(time_streams[0].reshape(NDET, block_count, WIN) * live_mask) * live_mask
    weight = lags[:, 0][:, None, None] * live_mask
    components = jnp.stack(
        [
            filtered,
            filtered * cosine,
            filtered * sine_term,
            weight,
            weight * cosine,
            weight * sine_term,
            weight * cosine * cosine,
            weight * cosine * sine_term,
            weight * sine_term * sine_term,
        ],
        axis=2,
    )
    initial = to_owner_blocks(bin_samples(components))
    right_side = initial[:, :3]
    weights = initial[:, 3:]
    solution = jnp.zeros_like(right_side)
    residual = right_side
    descent = precondition(weights, residual)
    direction = descent
    product_now = global_dot(residual, descent)
    for iteration in range(ITERS):
        from_whole_map = lax.all_gather(direction, "det", axis=0, tiled=True)
        from_grouped = from_whole_map.reshape(det_count, BPD, 3 * BLK)
        picked = jnp.einsum("ocb,obx->ocx", place_pick, from_grouped, precision=highest)
        fetched = picked.reshape(hit_total, 3, BLK)
        apply_per_block = jnp.dot(
            slot_pick.T, fetched.reshape(hit_total, 3 * BLK), precision=highest
        )
        apply_per_block = apply_per_block.reshape(NDET, block_count, 3, BLK)
        values = jnp.einsum("djwp,djcp->djcw", pixel_pick, apply_per_block, precision=highest)
        apply_signal = (
            values[:, :, 0] + values[:, :, 1] * cosine + values[:, :, 2] * sine_term
        ) * live_mask
        apply_filtered = noise_filter(apply_signal) * live_mask
        apply_components = jnp.stack(
            [apply_filtered, apply_filtered * cosine, apply_filtered * sine_term], axis=2
        )
        image_map = to_owner_blocks(bin_samples(apply_components))
        step_size = product_now / global_dot(direction, image_map)
        solution = solution + step_size * direction
        residual = residual - step_size * image_map
        descent = precondition(weights, residual)
        if iteration + 1 < ITERS:
            product_next = global_dot(residual, descent)
            direction = descent + product_next / product_now * direction
            product_now = product_next
    return (solution, descent)


def solution(mesh):
    in_specs = (
        P("det", None, "tm"),
        P("det", None, "tm"),
        P("det", None, "tm"),
        P("det", None, "tm"),
        P("det", None),
        P("det", None),
        P("det", None, None),
        P("det", None),
    )
    out_specs = (P("det", None, None), P("det", None, None))
    return jax.shard_map(
        per_device, mesh=mesh, in_specs=in_specs, out_specs=out_specs, check_vma=False
    )
```

profile of v0, /device:TPU:1, one launch (start us, length us, event | category | flops | bytes accessed | tf_op | source)
XLA Modules:
  0.0 1986.2 jit_solution(1493701683084729770)
XLA Ops:
  8.6 3.9 collective-permute-start
  48.3 1.5 multiply_reduce_fusion.39
  57.0 1.5 multiply_reduce_fusion.33
  113.4 583.8 %gather_fusion = f32[98304]{0:T(1024)S(1)} fusion(f32[65]{0:T(128)S(1)} %bitcast_dynamic-update-slice_fusion, s32[98304]{0:T(1024)S(1)} %broadcast_clamp_fusion), kind=kCustom, calls=%fused_computation | custom fusion | bytes 1179648 | tf_op jit(solution)/shard_map/gather | solution.py:54
  701.8 7.9 fusion
  709.7 12.7 reshape.851
  722.4 14.9 copy.43
  737.3 156.0 %reduce-scatter.2.cloned.1.call-done = f32[16,9,256]{2,0,1:T(8,128)} async-done(((f32[1024,9,256]{2,0,1:T(8,128)}), f32[16,9,256]{2,0,1:T(8,128)}) %reduce-scatter.2.cloned.1.call-update) | async-done | bytes 147472 | tf_op jit(solution)/shard_map/reduce_scatter | solution.py:138
  893.6 49.2 %all-reduce.10.cloned.1.call-done = f32[16,9,256]{2,0,1:T(8,128)} async-done(((f32[16,9,256]{2,0,1:T(8,128)}), f32[16,9,256]{2,0,1:T(8,128)}) %all-reduce.10.cloned.1.call-update) | async-done | bytes 147472 | tf_op jit(solution)/shard_map/psum | solution.py:139
  948.4 80.5 %all-gather.3.cloned.1.call-done = f32[1024,3,256]{2,0,1:T(8,128)} async-done(((f32[16,3,256]{2,0,1:T(8,128)}), f32[1024,3,256]{2,0,1:T(8,128)}) %all-gather.3.cloned.1.call-update) | async-done | bytes 3145744 | tf_op jit(solution)/shard_map/all_gather | solution.py:167
  1028.9 6.0 copy.44
  1034.9 4.8 reshape.852
  1039.7 2.0 fusion.33
  1045.4 3.1 collective-permute-start.2
  1049.9 2.9 collective-permute-done.3
  1056.8 2.9 fusion.16
  1059.7 3.3 reshape.858
  1064.9 191.2 %all-reduce.12.cloned.1.call-done = f32[1024,3,256]{2,1,0:T(4,128)} async-done(((f32[1024,3,256]{2,1,0:T(4,128)}), f32[1024,3,256]{2,1,0:T(4,128)}) %all-reduce.12.cloned.1.call-update) | async-done | bytes 3145744
  1257.0 13.5 psum.51
  1271.2 130.2 %all-reduce.5 = (f32[]{:T(128)}, f32[]{:T(128)}) all-reduce(f32[]{:T(128)} %get-tuple-element.19, f32[]{:T(128)} %get-tuple-element.18), channel_id=1, replica_groups=mesh['det'=64,'tm'=4] {'det'}, use_global_device_ids=true, to_apply=%region_68.69 | all-reduce | flops 2 | bytes 16 | tf_op jit(solution)/shard_map/psum | solution.py:85
  1404.0 124.6 %psum.53 = f32[]{:T(128)} all-reduce(f32[]{:T(128)} %multiply_reduce_fusion.1), channel_id=1, replica_groups=mesh['det'=64,'tm'=4] {'det'}, use_global_device_ids=true, to_apply=%region_74.75 | all-reduce | flops 1 | bytes 8 | tf_op jit(solution)/shard_map/psum | solution.py:85
  1530.8 73.7 %all-gather.5.cloned.1.call-done = f32[1024,3,256]{2,0,1:T(8,128)} async-done(((f32[16,3,256]{2,0,1:T(8,128)}), f32[1024,3,256]{2,0,1:T(8,128)}) %all-gather.5.cloned.1.call-update) | async-done | bytes 3145744 | tf_op jit(solution)/shard_map/all_gather | solution.py:167
  1604.5 6.0 copy.50
  1610.5 4.8 reshape.859
  1615.3 2.0 fusion.32
  1621.0 3.1 collective-permute-start.4
  1625.6 2.9 collective-permute-done.5
  1632.4 2.9 fusion.14
  1635.3 3.3 reshape.865
  1638.7 192.7 %all-reduce.14.cloned.1.call-done = f32[1024,3,256]{2,1,0:T(4,128)} async-done(((f32[1024,3,256]{2,1,0:T(4,128)}), f32[1024,3,256]{2,1,0:T(4,128)}) %all-reduce.14.cloned.1.call-update) | async-done | bytes 3145744
  1832.3 13.5 psum.54
  1846.5 130.2 %psum.55 = f32[]{:T(128)} all-reduce(f32[]{:T(128)} %multiply_reduce_fusion), channel_id=1, replica_groups=mesh['det'=64,'tm'=4] {'det'}, use_global_device_ids=true, to_apply=%region_78.79 | all-reduce | flops 1 | bytes 8 | tf_op jit(solution)/shard_map/psum | solution.py:85
  (276 shorter events, 130.4 us)
Async XLA Ops:
  7.2 886.2 %reduce-scatter.2.cloned.1.call-start = ((), (), s32[]{:S(2)}) async-start(), calls=%async_computation.1 | async-start | bytes 9584640 | tf_op jit(solution)/shard_map/reduce_scatter | solution.py:138
  8.6 691.0 %collective-permute-start = (f32[1,64]{1,0:T(1,128)S(1)}, f32[1,64]{1,0:T(1,128)S(1)}, u32[]{:S(2)}, u32[]{:S(2)}) collective-permute-start(f32[1,64]{1,0:T(1,128)S(1)} %get-tuple-element.57), channel_id=1, source_target_pairs={{0,1},{1,2},{2,3},{4,5},{5,6},{6,7},{8,9},{9,10},{10,11},{12,13},{... | collective-permute-start | bytes 776 | tf_op jit(solution)/shard_map/ppermute | solution.py:27
  12.6 687.0 %collective-permute-start.1 = (f32[1,64]{1,0:T(1,128)S(1)}, f32[1,64]{1,0:T(1,128)S(1)}, u32[]{:S(2)}, u32[]{:S(2)}) collective-permute-start(f32[1,64]{1,0:T(1,128)S(1)} %get-tuple-element.56), channel_id=1, source_target_pairs={{1,0},{2,1},{3,2},{5,4},{6,5},{7,6},{9,8},{10,9},{11,10},{13,12},{... | collective-permute-start | bytes 776 | tf_op jit(solution)/shard_map/ppermute | solution.py:29
  107.8 592.1 %copy-start.44 = (s32[384]{0:T(512)}, s32[384]{0:T(512)S(1)}, u32[]{:S(2)}) copy-start(s32[384]{0:T(512)S(1)} %iota_add_fusion) | copy-start | bytes 4612
  107.8 593.2 %copy-start.41 = (s32[64,2]{0,1:T(2,128)}, s32[64,2]{0,1:T(2,128)S(1)}, u32[]{:S(2)}) copy-start(s32[64,2]{0,1:T(2,128)S(1)} %multiply_add_fusion.3) | copy-start | bytes 1540
  113.3 584.0 %copy-start.37 = (f32[1,1,1024]{2,1,0:T(1,128)S(1)}, f32[1,1,1024]{2,1,0:T(1,128)}, u32[]{:S(2)}) copy-start(f32[1,1,1024]{2,1,0:T(1,128)} %param.11) | copy-start | bytes 12292
  113.3 584.7 %copy-start.47 = (s32[1,128]{1,0:T(1,128)S(1)}, s32[1,128]{1,0:T(1,128)}, u32[]{:S(2)}) copy-start(s32[1,128]{1,0:T(1,128)} %param.14) | copy-start | bytes 1540
  113.3 585.6 %copy-start.45 = (s32[1,1,1024]{2,1,0:T(1,128)S(1)}, s32[1,1,1024]{2,1,0:T(1,128)}, u32[]{:S(2)}) copy-start(s32[1,1,1024]{2,1,0:T(1,128)} %param.12) | copy-start | bytes 12292
  113.3 587.6 %copy-start.38 = (s32[1,1,4]{2,1,0:T(1,128)S(1)}, s32[1,1,4]{2,1,0:T(1,128)}, u32[]{:S(2)}) copy-start(s32[1,1,4]{2,1,0:T(1,128)} %param.13) | copy-start | bytes 52
  737.3 205.5 %all-reduce.10.cloned.1.call-start = ((), (), s32[]{:S(2)}) async-start(), calls=%async_computation.2 | async-start | bytes 294912 | tf_op jit(solution)/shard_map/psum | solution.py:139
  893.3 135.6 %all-gather.3.cloned.1.call-start = ((), (), s32[]{:S(2)}) async-start(), calls=%async_computation.3 | async-start | bytes 3194880 | tf_op jit(solution)/shard_map/all_gather | solution.py:167
  948.4 307.7 %all-reduce.12.cloned.1.call-start = ((), (), s32[]{:S(2)}) async-start(), calls=%async_computation.5 | async-start | bytes 8388608
  1045.4 4.4 collective-permute-start.2
  1048.5 4.3 collective-permute-start.3
  1063.0 339.8 %copy-start.17 = (f32[16,1,256]{2,0,1:T(8,128)S(1)}, f32[16,1,256]{2,0,1:T(8,128)}, u32[]{:S(2)}) copy-start(f32[16,1,256]{2,0,1:T(8,128)} %copy-done.16) | copy-start | bytes 49156
  1063.0 339.8 %copy-start.21 = (f32[16,1,256]{2,0,1:T(8,128)S(1)}, f32[16,1,256]{2,0,1:T(8,128)}, u32[]{:S(2)}) copy-start(f32[16,1,256]{2,0,1:T(8,128)} %copy-done.20) | copy-start | bytes 49156
  1063.0 339.8 %copy-start.24 = (f32[16,1,256]{2,0,1:T(8,128)S(1)}, f32[16,1,256]{2,0,1:T(8,128)}, u32[]{:S(2)}) copy-start(f32[16,1,256]{2,0,1:T(8,128)} %copy-done.23) | copy-start | bytes 49156
  1063.0 339.8 %copy-start.27 = (f32[16,1,256]{2,0,1:T(8,128)S(1)}, f32[16,1,256]{2,0,1:T(8,128)}, u32[]{:S(2)}) copy-start(f32[16,1,256]{2,0,1:T(8,128)} %copy-done.26) | copy-start | bytes 49156
  1063.0 339.8 %copy-start.29 = (f32[16,1,256]{2,0,1:T(8,128)S(1)}, f32[16,1,256]{2,0,1:T(8,128)}, u32[]{:S(2)}) copy-start(f32[16,1,256]{2,0,1:T(8,128)} %get-tuple-element.26) | copy-start | bytes 49156
  1063.0 339.8 %copy-start.31 = (f32[16,1,256]{2,0,1:T(8,128)S(1)}, f32[16,1,256]{2,0,1:T(8,128)}, u32[]{:S(2)}) copy-start(f32[16,1,256]{2,0,1:T(8,128)} %get-tuple-element.30) | copy-start | bytes 49156
  1063.0 339.8 %copy-start.33 = (f32[16,1,256]{2,0,1:T(8,128)S(1)}, f32[16,1,256]{2,0,1:T(8,128)}, u32[]{:S(2)}) copy-start(f32[16,1,256]{2,0,1:T(8,128)} %get-tuple-element.33) | copy-start | bytes 49156
  1063.1 541.4 %all-gather.5.cloned.1.call-start = ((), (), s32[]{:S(2)}) async-start(), calls=%async_computation.4 | async-start | bytes 3194880 | tf_op jit(solution)/shard_map/all_gather | solution.py:167
  1530.5 300.9 %all-reduce.14.cloned.1.call-start = ((), (), s32[]{:S(2)}) async-start(), calls=%async_computation.6 | async-start | bytes 8388608
  1621.0 4.4 collective-permute-start.4
  1624.1 4.3 collective-permute-start.5
  1638.6 340.1 %copy-start.18 = (f32[16,1,256]{2,0,1:T(8,128)S(1)}, f32[16,1,256]{2,0,1:T(8,128)}, u32[]{:S(2)}) copy-start(f32[16,1,256]{2,0,1:T(8,128)} %copy-done.16) | copy-start | bytes 49156
  1638.6 340.1 %copy-start.22 = (f32[16,1,256]{2,0,1:T(8,128)S(1)}, f32[16,1,256]{2,0,1:T(8,128)}, u32[]{:S(2)}) copy-start(f32[16,1,256]{2,0,1:T(8,128)} %copy-done.20) | copy-start | bytes 49156
  1638.6 340.1 %copy-start.25 = (f32[16,1,256]{2,0,1:T(8,128)S(1)}, f32[16,1,256]{2,0,1:T(8,128)}, u32[]{:S(2)}) copy-start(f32[16,1,256]{2,0,1:T(8,128)} %copy-done.23) | copy-start | bytes 49156
  1638.6 340.0 %copy-start.28 = (f32[16,1,256]{2,0,1:T(8,128)S(1)}, f32[16,1,256]{2,0,1:T(8,128)}, u32[]{:S(2)}) copy-start(f32[16,1,256]{2,0,1:T(8,128)} %copy-done.26) | copy-start | bytes 49156
  1638.6 340.0 %copy-start.30 = (f32[16,1,256]{2,0,1:T(8,128)S(1)}, f32[16,1,256]{2,0,1:T(8,128)}, u32[]{:S(2)}) copy-start(f32[16,1,256]{2,0,1:T(8,128)} %get-tuple-element.26) | copy-start | bytes 49156
  1638.7 340.0 %copy-start.32 = (f32[16,1,256]{2,0,1:T(8,128)S(1)}, f32[16,1,256]{2,0,1:T(8,128)}, u32[]{:S(2)}) copy-start(f32[16,1,256]{2,0,1:T(8,128)} %get-tuple-element.30) | copy-start | bytes 49156
  1638.7 340.0 %copy-start.34 = (f32[16,1,256]{2,0,1:T(8,128)S(1)}, f32[16,1,256]{2,0,1:T(8,128)}, u32[]{:S(2)}) copy-start(f32[16,1,256]{2,0,1:T(8,128)} %get-tuple-element.33) | copy-start | bytes 49156
  (29 other events, 2711.7 us)
Sparse Core Ops, SparseCore 0:
  737.4 155.8 reduce-scatter.1
  895.6 47.0 all-reduce.9
  948.5 80.3 all-gather.2
  1063.2 192.8 all-reduce.11
  1530.7 73.7 all-gather.4
  1638.8 192.5 all-reduce.13
where the time goes:
time: 1990 us
  waiting for transfers between devices  749 us (38%)
  local copies, waits for them, and re-layouts  649 us (33%)
  blocking collectives  412 us (21%)
  other arithmetic  107 us (5%)
  matrix products  30 us (2%)
  between operations  24.3 us (1%)
    gather x2, local copies, waits for them, and re-layouts, toeplitz_matrix(): return jnp.where(inside[None], lags[:, clipped], 0.0)  584 us
    psum x3, blocking collectives, global_dot(): return lax.psum(jnp.sum(left * right), 'det')  385 us
    unnamed x8, waiting for transfers between devices  384 us
    reduce_scatter x1, waiting for transfers between devices, to_owner_blocks(): lax.psum_scatter(whole_map, 'det', scatter_dimension=0, tiled=True)  156 us
    all_gather x2, waiting for transfers between devices, per_device(): from_whole_map = lax.all_gather(direction, 'det', axis=0, tiled=True)  154 us
    reduce_sum x64, other arithmetic, lag_table(): jnp.sum(filter_taps[..., :BAND + 1 - shift_lag] * filter_taps[..., shift_...  91.9 us
    psum x1, waiting for transfers between devices, to_owner_blocks(): owned_map = lax.psum(owned_map, 'tm')  49.2 us
  transfers between devices with their start and end apart: 12, of which 8 were waited for; matrix products, arithmetic and copies ran while one was open for 34% of the time, Pallas kernels for 0%

commit v1 on v0

v1 whole, which is shorter than its diff:
```python
import functools

import jax
import jax.numpy as jnp
from jax import lax
from jax.experimental import pallas as pl
from jax.experimental.pallas import tpu as pltpu
from jax.sharding import PartitionSpec as P

WIN = 256
BAND = 64
BPD = 16
HALF = 128
SPAN = 1024
BLOCKS = 4
DEVICES = 256
LABELS = DEVICES * BLOCKS

HIGHEST = lax.Precision.HIGHEST
NT = (((1,), (1,)), ((), ()))
MESH = pl.DeviceIdType.MESH

vmem = pl.BlockSpec(memory_space=pltpu.VMEM)
smem = pl.BlockSpec(memory_space=pltpu.SMEM)


def lanes(shape):
    return lax.broadcasted_iota(jnp.int32, shape, len(shape) - 1)


def rows_of(shape):
    return lax.broadcasted_iota(jnp.int32, shape, 0)


def band_filter(extended, band):
    turned = pltpu.roll(extended, HALF // 2, 1)
    keep = lanes((8, HALF)) < HALF // 2
    first = jnp.where(keep, turned[0:8], turned[1:9])
    second = jnp.where(keep, turned[1:9], turned[2:10])
    window = jnp.concatenate([first, second], axis=1)
    return jnp.dot(window, band, precision=HIGHEST, preferred_element_type=jnp.float32)


def grid_place():
    det = lax.axis_index("det")
    x = lax.axis_index("tm")
    return lax.div(det, 8), lax.rem(lax.div(det, 2), 4), lax.rem(det, 2), x


def device_at(z, y, core, x):
    return {"det": (z * 4 + y) * 2 + core, "tm": x}


def slot_of(z, y, core, x):
    major = y + core * (x - y)
    minor = x + core * (y - x)
    return ((core * 8 + z) * 4 + major) * 4 + minor


def meet():
    z, y, core, x = grid_place()
    barrier = pltpu.get_barrier_semaphore()
    peers = (
        [device_at(lax.rem(z + d, 8), y, core, x) for d in range(1, 8)]
        + [device_at(z, lax.rem(y + d, 4), core, x) for d in range(1, 4)]
        + [device_at(z, y, core, lax.rem(x + d, 4)) for d in range(1, 4)]
        + [device_at(z, y, 1 - core, x)]
    )
    for peer in peers:
        pl.semaphore_signal(barrier, inc=1, device_id=peer, device_id_type=MESH)
    pl.semaphore_wait(barrier, len(peers))


def exchange(sources, buffers, send_sems, recv_sems, local_sems):
    z, y, core, x = grid_place()
    a = y + core * (x - y)
    b = x + core * (y - x)

    def major_peer(step):
        return device_at(
            z,
            y + (1 - core) * (lax.rem(y + step, 4) - y),
            core,
            x + core * (lax.rem(x + step, 4) - x),
        )

    def minor_peer(step):
        return device_at(
            z,
            y + core * (lax.rem(y + step, 4) - y),
            core,
            x + (1 - core) * (lax.rem(x + step, 4) - x),
        )

    arrays = range(len(sources))

    def send(number, source_of, target_of, peer):
        copies = []
        for i in arrays:
            copy = pltpu.make_async_remote_copy(
                src_ref=source_of(i),
                dst_ref=target_of(i),
                send_sem=send_sems.at[i, number],
                recv_sem=recv_sems.at[i, number],
                device_id=peer,
                device_id_type=MESH,
            )
            copy.start()
            copies.append(copy)
        return copies

    def landed(copies):
        for copy in copies:
            copy.wait_recv()

    started = []
    keep = [
        pltpu.make_async_copy(sources[i], buffers[i].at[core, z, a, b], local_sems.at[i])
        for i in arrays
    ]
    first = [
        send(
            d - 1,
            lambda i: sources[i],
            lambda i: buffers[i].at[core, z, a, b],
            device_at(lax.rem(z + d, 8), y, core, x),
        )
        for d in (4, 3, 5, 2, 6, 1, 7)
    ]
    for copy in keep:
        copy.start()
    for copy in keep:
        copy.wait()
    for copies in first:
        landed(copies)
    started += first

    def column(i):
        return buffers[i].at[core, :, a, b]

    second = [send(6 + d, column, column, major_peer(d)) for d in (2, 1, 3)]
    for copies in second:
        landed(copies)
    started += second

    def part(number, half):
        depth = pl.ds(4 * half, 4)
        return lambda i: buffers[i].at[core, depth, :, number]

    def whole(number):
        return lambda i: buffers[i].at[core, :, :, number]

    after = minor_peer(1)
    before = minor_peer(3)
    partner = device_at(z, y, 1 - core, x)
    left = lax.rem(b + 3, 4)
    right = lax.rem(b + 1, 4)
    far = lax.rem(b + 2, 4)
    up = [send(10, part(b, 0), part(b, 0), after)]
    down = [send(12, part(b, 1), part(b, 1), before)]
    up.append(send(11, part(b, 1), part(b, 1), after))
    down.append(send(13, part(b, 0), part(b, 0), before))
    swaps = [send(16, whole(b), whole(b), partner)]
    landed(up[0])
    up.append(send(14, part(left, 0), part(left, 0), after))
    landed(down[0])
    down.append(send(15, part(right, 1), part(right, 1), before))
    landed(up[1])
    swaps.append(send(17, whole(left), whole(left), partner))
    landed(down[1])
    swaps.append(send(18, whole(right), whole(right), partner))
    landed(up[2])
    landed(down[2])
    swaps.append(send(19, whole(far), whole(far), partner))
    for copies in swaps:
        landed(copies)
    started += up + down + swaps
    for copies in started:
        for copy in copies:
            copy.wait_send()


EXCHANGE_SCRATCH = [
    pltpu.SemaphoreType.DMA((2, 20)),
    pltpu.SemaphoreType.DMA((2, 20)),
    pltpu.SemaphoreType.DMA((2,)),
]


def gather_kernel(values, meta, values_out, meta_out, send_sems, recv_sems, local_sems):
    meet()
    exchange([values, meta], [values_out, meta_out], send_sems, recv_sems, local_sems)


def prepare_kernel(
    valid, slots, hits, white, taps, stream, angle, offset,
    message_out, meta_out, base_out, band,
    hold, taps_row, message, meta, send_sems, recv_sems, local_sems, halo_send, halo_recv,
):
    meet()
    z, y, core, x = grid_place()
    tm = x
    halos = [
        pltpu.make_async_remote_copy(
            src_ref=stream.at[pl.ds(7, 1)],
            dst_ref=hold.at[0],
            send_sem=halo_send.at[0],
            recv_sem=halo_recv.at[0],
            device_id=device_at(z, y, core, lax.rem(x + 1, 4)),
            device_id_type=MESH,
        ),
        pltpu.make_async_remote_copy(
            src_ref=stream.at[pl.ds(0, 1)],
            dst_ref=hold.at[1],
            send_sem=halo_send.at[1],
            recv_sem=halo_recv.at[1],
            device_id=device_at(z, y, core, lax.rem(x + 3, 4)),
            device_id_type=MESH,
        ),
    ]
    for copy in halos:
        copy.start()
    cosine = jnp.cos(2.0 * angle[...])
    sine = jnp.sin(2.0 * angle[...])
    place_of = offset[...].astype(jnp.float32)
    for block in range(BLOCKS):
        for half in range(2):
            row = 2 * block + half
            for part, values in enumerate((cosine, sine, place_of)):
                at = 8 * block + 4 * half + part + 1
                message[at : at + 1, :] = values[row : row + 1]
    taps_row[...] = jnp.zeros_like(taps_row)
    taps_row[:, : BAND + 1] = taps[...]
    spread = jnp.broadcast_to(taps_row[...], (WIN, WIN))
    shifted = pltpu.roll(spread, HALF, 1, stride=1, stride_axis=0)
    lag_row = lax.dot_general(
        spread[:8], shifted, NT, precision=HIGHEST, preferred_element_type=jnp.float32
    )
    lag_row = lag_row + jnp.where(lanes((8, WIN)) == HALF, white[0], 0.0)
    table = pltpu.roll(
        jnp.broadcast_to(lag_row[0:1], (WIN, WIN)), WIN - HALF - BAND, 1, stride=1, stride_axis=0
    )
    band[...] = table[:, :HALF]
    lag_zero = lag_row[0:1, HALF : HALF + 1]

    remaining = valid[0] - tm * SPAN
    lane = lanes((1, HALF))
    header = jnp.where(lane == 8, jnp.broadcast_to(lag_zero, (1, HALF)), 0.0)
    for block in range(BLOCKS):
        found = hits[slots[block]].astype(jnp.float32)
        count = jnp.clip(remaining - block * WIN, 0, WIN).astype(jnp.float32)
        header = jnp.where(lane == block, found, header)
        header = jnp.where(lane == 4 + block, count, header)
    meta[...] = header

    for copy in halos:
        copy.wait_recv()
    extended = jnp.concatenate(
        [hold[0], stream[...], hold[1], jnp.zeros((6, HALF), jnp.float32)], axis=0
    )
    place = (rows_of((16, HALF)) - 1) * HALF + lanes((16, HALF))
    extended = jnp.where((place < remaining) & (place + tm * SPAN >= 0), extended, 0.0)
    own_live = rows_of((8, HALF)) * HALF + lanes((8, HALF)) < remaining
    filtered = jnp.where(own_live, band_filter(extended, table[:, :HALF]), 0.0)
    for block in range(BLOCKS):
        for half in range(2):
            row = 2 * block + half
            at = 8 * block + 4 * half
            message[at : at + 1, :] = filtered[row : row + 1]
    base_out[...] = filtered
    exchange([message, meta], [message_out, meta_out], send_sems, recv_sems, local_sems)
    for copy in halos:
        copy.wait_send()


def split_rows(values):
    high = values.astype(jnp.bfloat16)
    rest = values - high.astype(jnp.float32)
    middle = rest.astype(jnp.bfloat16)
    low = (rest - middle.astype(jnp.float32)).astype(jnp.bfloat16)
    return jnp.concatenate([high, middle, low], axis=0)


def wide(tile, row):
    return jnp.concatenate([tile[row : row + 1], tile[row + 4 : row + 5]], axis=1)


def match_sum(column, places, values):
    count = values.shape[0]
    picked = jnp.where(column == places, 1.0, 0.0).astype(jnp.bfloat16)
    out = lax.dot_general(split_rows(values), picked, NT, preferred_element_type=jnp.float32)
    return out[:count] + out[count : 2 * count] + out[2 * count :]


def weight_rows(weight, cosine, sine):
    first = weight * cosine
    second = weight * sine
    return [weight, first, second, first * cosine, first * sine, second * sine]


def own_labels():
    z, y, core, x = grid_place()
    own = slot_of(z, y, core, x) * BLOCKS
    before = slot_of(z, y, core, jnp.maximum(x - 1, 0)) * BLOCKS + BLOCKS - 1
    after = slot_of(z, y, core, jnp.minimum(x + 1, 3)) * BLOCKS
    usable = [jnp.minimum(x, 1)] + [1] * BLOCKS + [jnp.minimum(3 - x, 1)]
    return [before] + [own + block for block in range(BLOCKS)] + [after], usable


def own_columns(labels, gathered):
    rows = []
    for seg in range(6):
        tile = gathered[labels[seg]]
        rows += [tile[3:4], tile[7:8]]
    rows.append(jnp.zeros((HALF - 12, HALF), jnp.float32))
    turned = jnp.concatenate(rows, axis=0).T
    return [
        jnp.concatenate([turned[:, 2 * s : 2 * s + 1], turned[:, 2 * s + 1 : 2 * s + 2]], axis=0)
        for s in range(6)
    ]


def adjugate(w1, w2, w3, w4, w5, w6):
    aa = 1.0 + w1
    bb = 1.0 + w4
    cc = 1.0 + w6
    m_aa = bb * cc - w5 * w5
    m_ab = w3 * w5 - w2 * cc
    m_ac = w2 * w5 - w3 * bb
    m_bb = aa * cc - w3 * w3
    m_bc = w2 * w3 - aa * w5
    m_cc = aa * bb - w2 * w2
    det = aa * m_aa + w2 * m_ab + w3 * m_ac
    return m_aa, m_ab, m_ac, m_bb, m_bc, m_cc, det


def rows_to_hold(signal, hold):
    hold[0:1] = signal[0:1, HALF:]
    for seg in range(1, 5):
        hold[2 * seg - 1 : 2 * seg] = signal[seg : seg + 1, :HALF]
        hold[2 * seg : 2 * seg + 1] = signal[seg : seg + 1, HALF:]
    hold[9:10] = signal[5:6, :HALF]


def total(values):
    return jnp.sum(jnp.sum(values, axis=1, keepdims=True), axis=0, keepdims=True)


def own_live_of(info):
    remaining = info[0] - lax.axis_index("tm") * SPAN
    return rows_of((8, HALF)) * HALF + lanes((8, HALF)) < remaining


def first_kernel(
    info, nexts, counts, lives, lag_zero, gathered, base, band,
    filtered_out, part_out, factors, signal_out, comps, hold,
):
    labels, flags = own_labels()
    columns = own_columns(labels, gathered)
    lane = lanes((1, WIN))
    comps[...] = jnp.zeros_like(comps)
    for seg in range(6):
        column = columns[seg]
        usable = flags[seg]

        def body(_, carry, column=column):
            label, acc = carry
            tile = gathered[label]
            f = wide(tile, 0)
            co = wide(tile, 1)
            si = wide(tile, 2)
            weight = jnp.where(lane < lives[label], lag_zero[label // BLOCKS], 0.0)
            values = jnp.concatenate(
                [f, f * co, f * si] + weight_rows(weight, co, si)
                + [jnp.zeros((7, WIN), jnp.float32)], axis=0,
            )
            return nexts[label], acc + match_sum(column, wide(tile, 3), values)

        start = labels[seg]
        _, acc = lax.fori_loop(
            0, counts[start] * usable, body, (start, jnp.zeros((16, WIN), jnp.float32))
        )
        for comp in range(9):
            comps[comp, seg : seg + 1, :] = acc[comp : comp + 1]
        tile = gathered[start]
        comps[9, seg : seg + 1, :] = wide(tile, 1)
        comps[10, seg : seg + 1, :] = wide(tile, 2)
        comps[11, seg : seg + 1, :] = jnp.where(lane < lives[start] * usable, 1.0, 0.0)
    m_aa, m_ab, m_ac, m_bb, m_bc, m_cc, det = adjugate(*(comps[c] for c in range(3, 9)))
    co, si, live = comps[9], comps[10], comps[11]
    scale = live / det
    q1 = (m_aa + m_ab * co + m_ac * si) * scale
    q2 = (m_ab + m_bb * co + m_bc * si) * scale
    q3 = (m_ac + m_bc * co + m_cc * si) * scale
    factors[0] = q1
    factors[1] = q2
    factors[2] = q3
    signal = q1 * comps[0] + q2 * comps[1] + q3 * comps[2]
    signal_out[...] = signal
    hold[...] = jnp.zeros_like(hold)
    rows_to_hold(signal, hold)
    filtered = jnp.where(own_live_of(info), band_filter(hold[...], band[...]), 0.0)
    filtered_out[...] = filtered
    own = hold[1:9]
    lane = lanes((1, HALF))
    part_out[...] = jnp.where(lane == 0, total(base[...] * own), 0.0) + jnp.where(
        lane == 1, total(filtered * own), 0.0
    )


def second_kernel(
    info, nexts, counts, gathered, second, parts, base, own_first, band, factors, signal_in,
    filtered_out, part_out, comps, hold,
):
    sums = jnp.sum(parts[...], axis=0, keepdims=True)
    alpha = sums[:, 0:1] / sums[:, 1:2]
    labels, flags = own_labels()
    columns = own_columns(labels, gathered)
    comps[...] = jnp.zeros_like(comps)
    for seg in range(6):
        column = columns[seg]

        def body(_, carry, column=column):
            label, acc = carry
            tile = gathered[label]
            pair = second[label]
            f = jnp.concatenate([pair[0:1], pair[1:2]], axis=1)
            values = jnp.concatenate(
                [f, f * wide(tile, 1), f * wide(tile, 2), jnp.zeros((13, WIN), jnp.float32)], axis=0
            )
            return nexts[label], acc + match_sum(column, wide(tile, 3), values)

        start = labels[seg]
        _, acc = lax.fori_loop(
            0, counts[start] * flags[seg], body, (start, jnp.zeros((16, WIN), jnp.float32))
        )
        for comp in range(3):
            comps[comp, seg : seg + 1, :] = acc[comp : comp + 1]
    change = factors[0] * comps[0] + factors[1] * comps[1] + factors[2] * comps[2]
    signal = signal_in[...] - alpha * change
    hold[...] = jnp.zeros_like(hold)
    rows_to_hold(signal, hold)
    filtered = jnp.where(own_live_of(info), band_filter(hold[...], band[...]), 0.0)
    filtered_out[...] = filtered
    own = hold[1:9]
    first = own_first[...]
    lane = lanes((1, HALF))
    part_out[...] = (
        jnp.where(lane == 0, total((base[...] - alpha * first) * own), 0.0)
        + jnp.where(lane == 1, total(filtered * own), 0.0)
        + jnp.where(lane == 2, total(first * own), 0.0)
    )


def last_kernel(
    heads, nexts, lives, lag_zero, gathered, second, third, parts_two, parts_three,
    solution_out, residual_out, comps,
):
    sums = jnp.sum(parts_two[...], axis=0, keepdims=True)
    product, curve = sums[:, 0:1], sums[:, 1:2]
    alpha = product / curve
    sums = jnp.sum(parts_three[...], axis=0, keepdims=True)
    product_next = sums[:, 0:1]
    beta = product_next / product
    curve_next = sums[:, 1:2] + 2.0 * beta * sums[:, 2:3] + beta * beta * curve
    alpha_next = product_next / curve_next
    column = rows_of((WIN, 1)).astype(jnp.float32)
    lane = lanes((1, WIN))
    for block in range(BPD):

        def body(_, carry):
            label, acc = carry
            tile = gathered[label]
            co = wide(tile, 1)
            si = wide(tile, 2)
            pair = second[label]
            trio = third[label]
            rows = []
            for f in (
                wide(tile, 0),
                jnp.concatenate([pair[0:1], pair[1:2]], axis=1),
                jnp.concatenate([trio[0:1], trio[1:2]], axis=1),
            ):
                rows += [f, f * co, f * si]
            weight = jnp.where(lane < lives[label], lag_zero[label // BLOCKS], 0.0)
            values = jnp.concatenate(
                rows + weight_rows(weight, co, si) + [jnp.zeros((1, WIN), jnp.float32)], axis=0
            )
            return nexts[label], acc + match_sum(column, wide(tile, 3), values)

        _, acc = lax.fori_loop(
            0, heads[BPD + block], body, (heads[block], jnp.zeros((16, WIN), jnp.float32))
        )
        for comp in range(15):
            comps[comp, block : block + 1, :] = acc[comp : comp + 1]
    m_aa, m_ab, m_ac, m_bb, m_bc, m_cc, det = adjugate(*(comps[c] for c in range(9, 15)))

    def solve(r1, r2, r3):
        return (
            (m_aa * r1 + m_ab * r2 + m_ac * r3) / det,
            (m_ab * r1 + m_bb * r2 + m_bc * r3) / det,
            (m_ac * r1 + m_bc * r2 + m_cc * r3) / det,
        )

    right = [comps[c] for c in range(3)]
    image = [comps[3 + c] for c in range(3)]
    other = [comps[6 + c] for c in range(3)]
    residual = [r - alpha * w for r, w in zip(right, image)]
    start = solve(*right)
    middle = solve(*residual)
    direction = [m + beta * s for m, s in zip(middle, start)]
    final = solve(
        *(r - alpha_next * (v + beta * w) for r, v, w in zip(residual, other, image))
    )
    for comp in range(3):
        answer = alpha * start[comp] + alpha_next * direction[comp]
        solution_out[comp] = answer
        residual_out[comp] = final[comp]


def f32(*shape):
    return jax.ShapeDtypeStruct(shape, jnp.float32)


def gathered_shape(rows):
    return f32(2, 8, 4, 4, rows, HALF)


def gather_rows(values, part, number):
    rows, parts = pl.pallas_call(
        gather_kernel,
        out_shape=(gathered_shape(8), gathered_shape(1)),
        in_specs=[vmem] * 2,
        out_specs=(vmem,) * 2,
        scratch_shapes=EXCHANGE_SCRATCH,
        compiler_params=pltpu.CompilerParams(collective_id=number, has_side_effects=True),
        name="gather",
    )(values, part)
    return rows.reshape(LABELS, 2, HALF), parts.reshape(DEVICES, HALF)


def per_device(
    time_streams, pol_angle, offsets, block_slots, hit_ids, valid_counts, filter_taps, white_weight
):
    valid = valid_counts.reshape(1)
    message, metas, base, band = pl.pallas_call(
        prepare_kernel,
        out_shape=(gathered_shape(32), gathered_shape(1), f32(8, HALF), f32(WIN, HALF)),
        in_specs=[smem] * 4 + [vmem] * 4,
        out_specs=(vmem,) * 4,
        scratch_shapes=[
            pltpu.VMEM((2, 1, HALF), jnp.float32),
            pltpu.VMEM((1, WIN), jnp.float32),
            pltpu.VMEM((32, HALF), jnp.float32),
            pltpu.VMEM((1, HALF), jnp.float32),
        ]
        + EXCHANGE_SCRATCH
        + [pltpu.SemaphoreType.DMA((2,)), pltpu.SemaphoreType.DMA((2,))],
        compiler_params=pltpu.CompilerParams(collective_id=0, has_side_effects=True),
        name="prepare",
    )(
        valid, block_slots.reshape(BLOCKS), hit_ids.reshape(-1), white_weight.reshape(1),
        filter_taps.reshape(1, BAND + 1), time_streams.reshape(8, HALF), pol_angle.reshape(8, HALF),
        offsets.reshape(8, HALF),
    )
    gathered = message.reshape(LABELS, 8, HALF)
    metas = metas.reshape(DEVICES, HALF)

    blocks = metas[:, 0:4].reshape(LABELS)
    lives = metas[:, 4:8].reshape(LABELS).astype(jnp.int32)
    lag_zero = metas[:, 8]
    order = jnp.arange(LABELS, dtype=jnp.int32)
    same = blocks[:, None] == blocks[None, :]
    ahead = (order[None, :] - order[:, None] - 1) % LABELS
    nexts = (order + 1 + jnp.min(jnp.where(same, ahead, LABELS), axis=1)) % LABELS
    counts = jnp.sum(same, axis=1, dtype=jnp.int32)
    owned = (lax.axis_index("det") * BPD + jnp.arange(BPD, dtype=jnp.int32)).astype(jnp.float32)
    mine = owned[:, None] == blocks[None, :]
    heads = jnp.concatenate(
        [
            jnp.min(jnp.where(mine, order[None, :], LABELS - 1), axis=1),
            jnp.sum(mine, axis=1, dtype=jnp.int32),
        ]
    )

    first, part_one, factors, signal = pl.pallas_call(
        first_kernel,
        out_shape=(f32(8, HALF), f32(1, HALF), f32(3, 8, WIN), f32(8, WIN)),
        in_specs=[smem] * 5 + [vmem] * 3,
        out_specs=(vmem,) * 4,
        scratch_shapes=[
            pltpu.VMEM((12, 8, WIN), jnp.float32),
            pltpu.VMEM((16, HALF), jnp.float32),
        ],
        name="first",
    )(valid, nexts, counts, lives, lag_zero, gathered, base, band)
    second, parts_two = gather_rows(first, part_one, 1)
    other, part_two = pl.pallas_call(
        second_kernel,
        out_shape=(f32(8, HALF), f32(1, HALF)),
        in_specs=[smem] * 3 + [vmem] * 8,
        out_specs=(vmem,) * 2,
        scratch_shapes=[
            pltpu.VMEM((3, 8, WIN), jnp.float32),
            pltpu.VMEM((16, HALF), jnp.float32),
        ],
        name="second",
    )(valid, nexts, counts, gathered, second, parts_two, base, first, band, factors, signal)
    third, parts_three = gather_rows(other, part_two, 2)
    answers = pl.pallas_call(
        last_kernel,
        out_shape=(f32(3, BPD, WIN), f32(3, BPD, WIN)),
        in_specs=[smem] * 4 + [vmem] * 5,
        out_specs=(vmem,) * 2,
        scratch_shapes=[pltpu.VMEM((15, BPD, WIN), jnp.float32)],
        name="last",
    )(heads, nexts, lives, lag_zero, gathered, second, third, parts_two, parts_three)
    return tuple(jnp.transpose(answer, (1, 0, 2)) for answer in answers)


def solution(mesh):
    in_specs = (
        P("det", None, "tm"),
        P("det", None, "tm"),
        P("det", None, "tm"),
        P("det", None, "tm"),
        P("det", None),
        P("det", None),
        P("det", None, None),
        P("det", None),
    )
    out_specs = (P("det", None, None), P("det", None, None))
    return jax.shard_map(
        per_device, mesh=mesh, in_specs=in_specs, out_specs=out_specs, check_vma=False
    )
```

time: 1990 us -> 121 us (0.06)
  waiting for transfers between devices: 749 us -> 0 us
  local copies, waits for them, and re-layouts: 649 us -> 2.45 us
  blocking collectives: 412 us -> 0 us
  Pallas kernels: 0 us -> 110 us
  other arithmetic: 107 us -> 6.33 us
  matrix products: 30 us -> 0 us
  between operations: 24.3 us -> 1.98 us
    gather x2 -> x0, local copies, waits for them, and re-layouts: 584 us -> none  [toeplitz_matrix(): return jnp.where(inside[None], lags[:, clipped], 0.0)]
    psum x5 -> x0, blocking collectives: 412 us -> none  [the longest x3 385 us: global_dot(): return lax.psum(jnp.sum(left * right), 'det')]
    unnamed x8 -> x0, waiting for transfers between devices: 384 us -> none
    reduce_scatter x1 -> x0, waiting for transfers between devices: 156 us -> none  [to_owner_blocks(): lax.psum_scatter(whole_map, 'det', scatter_dimension=0, tiled=True)]
    all_gather x2 -> x0, waiting for transfers between devices: 154 us -> none  [per_device(): from_whole_map = lax.all_gather(direction, 'det', axis=0, tiled=True)]
    pallas_call x0 -> x6, Pallas kernels: none -> 110 us  [the longest x2 50.1 us: gather_rows(): pl.pallas_call(gather_kernel, out_shape=(gathered_shape(8), gathered_shap...]
    reduce_sum x67 -> x1, other arithmetic: 93.7 us -> 3.85 us  [per_device(): counts = jnp.sum(same, axis=1, dtype=jnp.int32)]
    psum x1 -> x0, waiting for transfers between devices: 49.2 us -> none  [to_owner_blocks(): owned_map = lax.psum(owned_map, 'tm')]
  transfers between devices with their start and end apart: 12 -> 0, of which waited for: 8 -> 0; matrix products, arithmetic and copies ran while one was open for 34% -> 0% of each run, Pallas kernels for 0% -> 0%
where the time goes in v1:
time: 121 us
  Pallas kernels  110 us (91%)
  other arithmetic  6.33 us (5%)
  local copies, waits for them, and re-layouts  2.45 us (2%)
  between operations  1.98 us (2%)
    pallas_call x2, Pallas kernels, gather_rows(): pl.pallas_call(gather_kernel, out_shape=(gathered_shape(8), gathered_shap...  50.1 us
    pallas_call x1, Pallas kernels, per_device(): pl.pallas_call(prepare_kernel, out_shape=(gathered_shape(32), gathered_sh...  42.2 us
    pallas_call x1, Pallas kernels, per_device(): pl.pallas_call(last_kernel, out_shape=(f32(3, BPD, WIN), f32(3, BPD, WIN)...  6.92 us
    pallas_call x1, Pallas kernels, per_device(): pl.pallas_call(second_kernel, out_shape=(f32(8, HALF), f32(1, HALF)), in_...  5.53 us
    pallas_call x1, Pallas kernels, per_device(): pl.pallas_call(first_kernel, out_shape=(f32(8, HALF), f32(1, HALF), f32(3...  5.26 us
    reduce_sum x1, other arithmetic, per_device(): counts = jnp.sum(same, axis=1, dtype=jnp.int32)  3.85 us

profile of v1, /device:TPU:1, one launch (start us, length us, event | category | flops | bytes accessed | tf_op | source)
XLA Modules:
  0.0 120.7 jit_solution(2927554638382447534)
XLA Ops:
  1.9 42.2 %prepare.1 = (f32[2,8,4,4,32,128]{5,4,3,2,1,0:T(8,128)}, f32[2,8,4,4,1,128]{5,4,3,2,1,0:T(1,128)}, f32[8,128]{1,0:T(8,128)}, f32[256,128]{1,0:T(8,128)}) custom-call(s32[1]{0:T(128)} %bitcast.17.valid, s32[4]{0:T(128)} %bitcast.37, s32[128]{0:T(128)} %bitcast.38, f32[1]{0:T(128)} %bitcast.20.white, f32[1,65]{1,0:T(1,128)} %bitcast.39, f32[8,128]{1,0:T(8,128)} %bitcast.34, ...), custom_call_target="tpu_custom_call" | custom-call | tf_op jit(solution)/shard_map/prepare/pallas_call | solution.py:546
  44.1 1.0 slice.14
  45.1 0.6 copy.12
  45.7 1.1 slice_convert_fusion
  46.8 0.7 convert_element_type.21.lives
  47.5 0.1 eq.33
  47.6 0.2 fusion.3
  47.8 0.6 pad_add_fusion.heads
  48.4 3.8 %fusion.1 = (s32[1024]{0:T(1024)}, s32[1024]{0:T(1024)S(1)}) fusion(f32[1024]{0:T(1024)S(1)} %eq.33), kind=kLoop, calls=%fused_computation.6 | loop fusion | flops 18872320 | bytes 12288 | tf_op jit(solution)/shard_map/reduce_sum | solution.py:576
  52.3 0.6 add_select_fusion.1.nexts
  52.9 5.3 %first.1 = (f32[8,128]{1,0:T(8,128)}, f32[1,128]{1,0:T(1,128)}, f32[3,8,256]{2,1,0:T(8,128)}, f32[8,256]{1,0:T(8,128)}) custom-call(s32[1]{0:T(128)} %bitcast.18.info, s32[1024]{0:T(1024)} %add_select_fusion.1.nexts, s32[1024]{0:T(1024)} %get-tuple-element.36.counts, s32[1024]{0:T(1024)} %convert_element_type.21.lives, f32[256]{0:T(256)} %bitcast.32, ...), custom_call_target="tpu_custom_call" | custom-call | tf_op jit(solution)/shard_map/first/pallas_call | solution.py:586
  58.1 25.2 %gather.2 = (f32[2,8,4,4,8,128]{5,4,3,2,1,0:T(8,128)}, f32[2,8,4,4,1,128]{5,4,3,2,1,0:T(1,128)}) custom-call(f32[8,128]{1,0:T(8,128)} %get-tuple-element.22.values.own_first, f32[1,128]{1,0:T(1,128)} %get-tuple-element.23.meta), custom_call_target="tpu_custom_call" | custom-call | tf_op jit(solution)/shard_map/gather/pallas_call | solution.py:530
  83.4 5.5 %second.1 = (f32[8,128]{1,0:T(8,128)}, f32[1,128]{1,0:T(1,128)}) custom-call(s32[1]{0:T(128)} %bitcast.19.info, s32[1024]{0:T(1024)} %add_select_fusion.1.nexts, s32[1024]{0:T(1024)} %get-tuple-element.36.counts, f32[1024,8,128]{2,1,0:T(8,128)} %bitcast.22, f32[1024,2,128]{2,1,0:T(2,128)} %bitcast.24, f32[256,128]{1,0:T(8,128)} %bitcast.29, ...), custom_call_target="tpu_custom_call" | custom-call | tf_op jit(solution)/shard_map/second/pallas_call | solution.py:598
  88.9 24.8 %gather.3 = (f32[2,8,4,4,8,128]{5,4,3,2,1,0:T(8,128)}, f32[2,8,4,4,1,128]{5,4,3,2,1,0:T(1,128)}) custom-call(f32[8,128]{1,0:T(8,128)} %get-tuple-element.28.values, f32[1,128]{1,0:T(1,128)} %get-tuple-element.29.meta), custom_call_target="tpu_custom_call" | custom-call | tf_op jit(solution)/shard_map/gather/pallas_call | solution.py:530
  113.7 6.9 %last.1 = (f32[3,16,256]{2,1,0:T(8,128)}, f32[3,16,256]{2,1,0:T(8,128)}) custom-call(s32[32]{0:T(128)} %pad_add_fusion.heads, s32[1024]{0:T(1024)} %add_select_fusion.1.nexts, s32[1024]{0:T(1024)} %convert_element_type.21.lives, f32[256]{0:T(256)} %bitcast.33, f32[1024,8,128]{2,1,0:T(8,128)} %bitcast.23, f32[1024,2,128]{2,1,0:T(2,128)} %bitcast.25, ...), custom_call_target="tpu_custom_call" | custom-call | tf_op jit(solution)/shard_map/last/pallas_call | solution.py:610
  (1 shorter events, 0.0 us)

commit v2 on v1

--- a/solution.py
+++ b/solution.py
@@ -14,6 +14,8 @@
 SPAN = 1024
 BLOCKS = 4
 DEVICES = 256
+PAIRS = 28
+SLOTS = 40
 LABELS = DEVICES * BLOCKS
 
 HIGHEST = lax.Precision.HIGHEST
@@ -518,6 +520,548 @@
         residual_out[comp] = final[comp]
 
 
+class Mover:
+    def __init__(self, source, buffer, sems, number):
+        self.source, self.buffer = source, buffer
+        self.send_sems, self.recv_sems, self.local_sems = sems
+        self.number = number
+        self.z, self.y, self.core, self.x = grid_place()
+        self.a = self.y + self.core * (self.x - self.y)
+        self.b = self.x + self.core * (self.y - self.x)
+        self.started = []
+
+    def major_peer(self, step):
+        z, y, core, x = self.z, self.y, self.core, self.x
+        return device_at(
+            z,
+            y + (1 - core) * (lax.rem(y + step, 4) - y),
+            core,
+            x + core * (lax.rem(x + step, 4) - x),
+        )
+
+    def minor_peer(self, step):
+        z, y, core, x = self.z, self.y, self.core, self.x
+        return device_at(
+            z,
+            y + core * (lax.rem(y + step, 4) - y),
+            core,
+            x + (1 - core) * (lax.rem(x + step, 4) - x),
+        )
+
+    def send(self, number, source, target, peer):
+        copy = pltpu.make_async_remote_copy(
+            src_ref=source,
+            dst_ref=target,
+            send_sem=self.send_sems.at[self.number, number],
+            recv_sem=self.recv_sems.at[self.number, number],
+            device_id=peer,
+            device_id_type=MESH,
+        )
+        copy.start()
+        self.started.append(copy)
+        return copy
+
+    def start_first(self):
+        z, y, core, x = self.z, self.y, self.core, self.x
+        own = self.buffer.at[core, z, self.a, self.b]
+        self.first = [
+            self.send(d - 1, self.source, own, device_at(lax.rem(z + d, 8), y, core, x))
+            for d in (4, 3, 5, 2, 6, 1, 7)
+        ]
+        self.keep = pltpu.make_async_copy(self.source, own, self.local_sems.at[self.number])
+        self.keep.start()
+
+    def start_second(self):
+        self.keep.wait()
+        for copy in self.first:
+            copy.wait_recv()
+        column = self.buffer.at[self.core, :, self.a, self.b]
+        self.second = [self.send(6 + d, column, column, self.major_peer(d)) for d in (2, 1, 3)]
+
+    def part(self, number, half):
+        return self.buffer.at[self.core, pl.ds(4 * half, 4), :, number]
+
+    def whole(self, number):
+        return self.buffer.at[self.core, :, :, number]
+
+    def pass_on(self, number, ref, peer):
+        return self.send(number, ref, ref, peer)
+
+    def start_small(self):
+        for copy in self.second:
+            copy.wait_recv()
+        self.third = [
+            self.pass_on(9 + d, self.whole(self.b), self.minor_peer(d)) for d in (2, 1, 3)
+        ]
+
+    def start_small_swap(self):
+        for copy in self.third:
+            copy.wait_recv()
+        partner = device_at(self.z, self.y, 1 - self.core, self.x)
+        self.swaps = [self.pass_on(16, self.buffer.at[self.core], partner)]
+
+    def start_third(self):
+        for copy in self.second:
+            copy.wait_recv()
+        self.after, self.before = self.minor_peer(1), self.minor_peer(3)
+        self.partner = device_at(self.z, self.y, 1 - self.core, self.x)
+        self.up = [self.pass_on(10, self.part(self.b, 0), self.after)]
+        self.down = [self.pass_on(12, self.part(self.b, 1), self.before)]
+        self.up.append(self.pass_on(11, self.part(self.b, 1), self.after))
+        self.down.append(self.pass_on(13, self.part(self.b, 0), self.before))
+        self.swaps = [self.pass_on(16, self.whole(self.b), self.partner)]
+
+    def forward(self):
+        left, right = lax.rem(self.b + 3, 4), lax.rem(self.b + 1, 4)
+        self.up[0].wait_recv()
+        self.up.append(self.pass_on(14, self.part(left, 0), self.after))
+        self.down[0].wait_recv()
+        self.down.append(self.pass_on(15, self.part(right, 1), self.before))
+
+    def near(self):
+        left, right = lax.rem(self.b + 3, 4), lax.rem(self.b + 1, 4)
+        self.up[1].wait_recv()
+        self.swaps.append(self.pass_on(17, self.whole(left), self.partner))
+        self.down[1].wait_recv()
+        self.swaps.append(self.pass_on(18, self.whole(right), self.partner))
+
+    def far(self):
+        far = lax.rem(self.b + 2, 4)
+        self.up[2].wait_recv()
+        self.down[2].wait_recv()
+        self.swaps.append(self.pass_on(19, self.whole(far), self.partner))
+
+    def arrive(self):
+        for copy in self.swaps:
+            copy.wait_recv()
+
+    def finish(self):
+        for copy in self.started:
+            copy.wait_send()
+
+
+def locate(label):
+    return (
+        lax.shift_right_logical(label, 9) & 1,
+        lax.shift_right_logical(label, 6) & 7,
+        lax.shift_right_logical(label, 4) & 3,
+        lax.shift_right_logical(label, 2) & 3,
+        label & 3,
+    )
+
+
+def joined(tile):
+    return jnp.concatenate([tile[0:1], tile[1:2]], axis=1)
+
+
+def split_product(rows, picked):
+    count = len(rows)
+    values = jnp.concatenate(rows, axis=0)
+    high = values.astype(jnp.bfloat16).astype(jnp.float32)
+    rest = values - high
+    middle = rest.astype(jnp.bfloat16).astype(jnp.float32)
+    low = rest - middle
+    pad = -3 * count % 16
+    stack = [high, middle, low]
+    if pad:
+        stack.append(jnp.zeros((pad, WIN), jnp.float32))
+    left = jnp.concatenate(stack, axis=0).astype(jnp.bfloat16)
+    out = lax.dot_general(left, picked, NT, preferred_element_type=jnp.float32)
+    return [
+        out[c : c + 1] + out[count + c : count + c + 1] + out[2 * count + c : 2 * count + c + 1]
+        for c in range(count)
+    ]
+
+
+def matches(column, places):
+    low = jnp.where(column == places[0:1], 1.0, 0.0)
+    high = jnp.where(column == places[1:2], 1.0, 0.0)
+    return jnp.concatenate([low, high], axis=1).astype(jnp.bfloat16)
+
+
+def make_lists(metas, list_a, list_b, live_a, live_b, lag_a, lag_b):
+    z, y, core, x = grid_place()
+    labels, usable = own_labels()
+    table = metas[...].reshape(DEVICES, HALF).T
+    blocks = jnp.concatenate(
+        [table[j : j + 1, HALF * h : HALF * h + HALF] for j in range(4) for h in range(2)], axis=0
+    )
+    lives = jnp.concatenate(
+        [table[4 + j : 5 + j, HALF * h : HALF * h + HALF] for j in range(4) for h in range(2)], axis=0
+    )
+    lags = jnp.concatenate(
+        [table[8:9, HALF * h : HALF * h + HALF] for _ in range(4) for h in range(2)], axis=0
+    )
+    row = rows_of((8, HALF))
+    label = (((row & 1) * HALF + lanes((8, HALF))) * 4 + lax.shift_right_logical(row, 1)).astype(
+        jnp.float32
+    )
+    masks = []
+    for seg in range(6):
+        c, zz, a, b, _ = locate(labels[seg])
+        number = (3, 0, 1, 2, 3, 0)[seg]
+        own = metas[c, zz, a, b][:, number : number + 1]
+        flag = usable[seg] if isinstance(usable[seg], int) else usable[seg].astype(jnp.float32)
+        masks.append(jnp.where(blocks == own, 1.0, 0.0) * flag)
+    det = lax.axis_index("det")
+    base = (det * BPD).astype(jnp.float32)
+    masks.append(jnp.where((blocks >= base) & (blocks < base + BPD), 1.0, 0.0))
+    masks.append(jnp.zeros((8, HALF), jnp.float32))
+    mask = jnp.concatenate(masks, axis=0)
+    ahead = jnp.where(rows_of((HALF, HALF)) < lanes((HALF, HALF)), 1.0, 0.0)
+    within = jnp.dot(mask, ahead, precision=HIGHEST, preferred_element_type=jnp.float32)
+    totals = jnp.broadcast_to(jnp.sum(mask, axis=1, keepdims=True), (64, HALF))
+    above = jnp.where(
+        (rows_of((64, 64)) > lanes((64, 64))) & ((rows_of((64, 64)) >= 48) == (lanes((64, 64)) >= 48)),
+        1.0, 0.0,
+    )
+    rank = within + jnp.dot(above, totals, precision=HIGHEST, preferred_element_type=jnp.float32)
+    rank = jnp.where(mask > 0.0, rank, -1.0)
+    count_a = jnp.sum(totals[0:48, 0:1], axis=0, keepdims=True)
+    count_b = jnp.sum(totals[48:56, 0:1], axis=0, keepdims=True)
+    over = jnp.where((count_a > PAIRS) | (count_b > SLOTS), 1.0, 0.0)
+
+    def fill(rows, first, size, code_of, list_ref, live_ref, lag_ref):
+        wanted = rows_of((size, HALF)).astype(jnp.float32)
+        code = jnp.zeros((size, HALF), jnp.float32)
+        live = jnp.zeros((size, HALF), jnp.float32)
+        lag = jnp.zeros((size, HALF), jnp.float32)
+        for r in range(rows):
+            k = r % 8
+            hit = wanted == rank[first + r : first + r + 1]
+            code += jnp.where(hit, code_of(r), 0.0)
+            live += jnp.where(hit, lives[k : k + 1], 0.0)
+            lag += jnp.where(hit, lags[k : k + 1], 0.0)
+
+        def spread(values):
+            return jnp.broadcast_to(jnp.sum(values, axis=1, keepdims=True), (size, HALF))
+
+        list_ref[...] = spread(code).astype(jnp.int32)
+        live_ref[...] = spread(live)
+        lag_ref[...] = spread(lag)
+
+    fill(
+        48, 0, 32, lambda r: label[r % 8 : r % 8 + 1] * 8.0 + (r // 8 + 1.0), list_a, live_a, lag_a
+    )
+    fill(
+        8, 48, SLOTS, lambda r: label[r : r + 1] * 32.0 + (blocks[r : r + 1] - base + 1.0),
+        list_b, live_b, lag_b,
+    )
+    return over
+
+
+def whole_kernel(
+    valid, slots, hits, white, taps, stream, angle, offset,
+    solution_out, residual_out, over_out,
+    hold, taps_row, fixed, meta, base, message, row_two, message_two,
+    all_fixed, all_meta, all_base, all_first, meta_two, all_second, meta_three,
+    columns, picked_a, picked_b, trig_a, trig_b, list_a, list_b, live_a, live_b, lag_a, lag_b,
+    near_a, near_b, comps, owned, factors, halo_rows,
+    send_sems, recv_sems, local_sems, halo_send, halo_recv, list_sems,
+):
+    z, y, core, x = grid_place()
+    tm = x
+    barrier = pltpu.get_barrier_semaphore()
+    peers = (
+        [device_at(lax.rem(z + d, 8), y, core, x) for d in range(1, 8)]
+        + [device_at(z, lax.rem(y + d, 4), core, x) for d in range(1, 4)]
+        + [device_at(z, y, core, lax.rem(x + d, 4)) for d in range(1, 4)]
+        + [device_at(z, y, 1 - core, x)]
+    )
+    for peer in peers:
+        pl.semaphore_signal(barrier, inc=1, device_id=peer, device_id_type=MESH)
+
+    place_of = offset[...].astype(jnp.float32)
+    for block in range(BLOCKS):
+        fixed[block, 0:2, :] = angle[2 * block : 2 * block + 2]
+        fixed[block, 2:4, :] = place_of[2 * block : 2 * block + 2]
+    taps_row[...] = jnp.zeros_like(taps_row)
+    taps_row[:, : BAND + 1] = taps[...]
+    spread = jnp.broadcast_to(taps_row[...], (WIN, WIN))
+    shifted = pltpu.roll(spread, HALF, 1, stride=1, stride_axis=0)
+    lag_row = lax.dot_general(
+        spread[:8], shifted, NT, precision=HIGHEST, preferred_element_type=jnp.float32
+    )
+    lag_row = lag_row + jnp.where(lanes((8, WIN)) == HALF, white[0], 0.0)
+    band = pltpu.roll(
+        jnp.broadcast_to(lag_row[0:1], (WIN, WIN)), WIN - HALF - BAND, 1, stride=1, stride_axis=0
+    )[:, :HALF]
+    lag_zero = lag_row[0:1, HALF : HALF + 1]
+    remaining = valid[0] - tm * SPAN
+    lane = lanes((1, HALF))
+    header = jnp.where(lane == 8, jnp.broadcast_to(lag_zero, (1, HALF)), 0.0)
+    for block in range(BLOCKS):
+        found = hits[slots[block]].astype(jnp.float32)
+        count = jnp.clip(remaining - block * WIN, 0, WIN).astype(jnp.float32)
+        header = jnp.where(lane == block, found, header)
+        header = jnp.where(lane == 4 + block, count, header)
+    meta[...] = header
+    own_live = rows_of((8, HALF)) * HALF + lanes((8, HALF)) < remaining
+
+    pl.semaphore_wait(barrier, len(peers))
+    halos = [
+        pltpu.make_async_remote_copy(
+            src_ref=stream.at[pl.ds(at, 1)],
+            dst_ref=hold.at[i],
+            send_sem=halo_send.at[i],
+            recv_sem=halo_recv.at[i],
+            device_id=device_at(z, y, core, lax.rem(x + step, 4)),
+            device_id_type=MESH,
+        )
+        for i, (at, step) in enumerate(((7, 1), (0, 3)))
+    ]
+    for copy in halos:
+        copy.start()
+    sems = (send_sems, recv_sems, local_sems)
+    movers = [
+        Mover(fixed, all_fixed, sems, 0),
+        Mover(meta, all_meta, sems, 1),
+        Mover(base, all_base, sems, 2),
+        Mover(message, all_first, sems, 3),
+        Mover(row_two.at[0], meta_two, sems, 4),
+        Mover(message_two, all_second, sems, 5),
+        Mover(row_two.at[1], meta_three, sems, 6),
+    ]
+    big, small, mid = movers[:3]
+    small.start_first()
+    big.start_first()
+
+    for copy in halos:
+        copy.wait_recv()
+    extended = jnp.concatenate(
+        [hold[0], stream[...], hold[1], jnp.zeros((6, HALF), jnp.float32)], axis=0
+    )
+    place = (rows_of((16, HALF)) - 1) * HALF + lanes((16, HALF))
+    extended = jnp.where((place < remaining) & (place + tm * SPAN >= 0), extended, 0.0)
+    filtered = jnp.where(own_live, band_filter(extended, band), 0.0)
+    base_own = filtered
+    for block in range(BLOCKS):
+        base[block] = filtered[2 * block : 2 * block + 2]
+    mid.start_first()
+
+    small.start_second()
+    big.start_second()
+    mid.start_second()
+    small.start_small()
+    big.start_third()
+    mid.start_third()
+    small.start_small_swap()
+    small.arrive()
+    over = make_lists(all_meta, near_a, near_b, live_a, live_b, lag_a, lag_b)
+    copies = [
+        pltpu.make_async_copy(near_a, list_a, list_sems.at[0]),
+        pltpu.make_async_copy(near_b, list_b, list_sems.at[1]),
+    ]
+    for copy in copies:
+        copy.start()
+    big.forward()
+    mid.forward()
+    big.near()
+    mid.near()
+    big.far()
+    mid.far()
+    for copy in copies:
+        copy.wait()
+    comps[...] = jnp.zeros_like(comps)
+    owned[...] = jnp.zeros_like(owned)
+    big.arrive()
+    mid.arrive()
+
+    labels, usable = own_labels()
+    rows = []
+    for seg in range(6):
+        tile = all_fixed[locate(labels[seg])]
+        rows.append(tile[2:4])
+        turn = 2.0 * tile[0:2]
+        comps[9, seg : seg + 1, :] = joined(jnp.cos(turn))
+        comps[10, seg : seg + 1, :] = joined(jnp.sin(turn))
+    rows.append(jnp.zeros((HALF - 12, HALF), jnp.float32))
+    turned = jnp.concatenate(rows, axis=0).T
+    for seg in range(6):
+        for half in range(2):
+            at = 2 * seg + half
+            columns[seg, HALF * half : HALF * half + HALF, :] = jnp.broadcast_to(
+                turned[:, at : at + 1], (HALF, HALF)
+            )
+    wide_lane = lanes((1, WIN)).astype(jnp.float32)
+
+    def doubled(row):
+        return jnp.concatenate([row, row], axis=1)
+
+    def nine(p, where_at, trig, live, lag):
+        tile = all_fixed[where_at]
+        turn = 2.0 * tile[0:2]
+        co2, si2 = jnp.cos(turn), jnp.sin(turn)
+        trig[p, 0:2, :] = co2
+        trig[p, 2:4, :] = si2
+        co, si = joined(co2), joined(si2)
+        f = joined(all_base[where_at])
+        weight = jnp.where(
+            wide_lane < doubled(live[pl.ds(p, 1), :]), doubled(lag[pl.ds(p, 1), :]), 0.0
+        )
+        return tile[2:4], [f, f * co, f * si] + weight_rows(weight, co, si)
+
+    def pair_first(p, carry):
+        code = list_a[p, 0]
+        seg = (code & 7) - 1
+        places, values = nine(
+            p, locate(lax.shift_right_logical(code, 3)), trig_a, live_a, lag_a
+        )
+        picked = matches(columns[jnp.clip(seg, 0, 5)], places)
+        picked_a[p] = picked
+        here = rows_of((8, WIN)) == seg
+        for c, value in enumerate(split_product(values, picked)):
+            comps[c] += jnp.where(here, value, 0.0)
+        return carry
+
+    lax.fori_loop(0, PAIRS, pair_first, 0, unroll=2)
+    m_aa, m_ab, m_ac, m_bb, m_bc, m_cc, det = adjugate(*(comps[c] for c in range(3, 9)))
+    co, si = comps[9], comps[10]
+    seg_row = rows_of((8, WIN))
+    time = tm * SPAN + (seg_row - 1) * WIN + lanes((8, WIN))
+    live = (time >= 0) & (time < valid[0]) & (seg_row < 6)
+    scale = jnp.where(live, 1.0, 0.0) / det
+    factors[0] = (m_aa + m_ab * co + m_ac * si) * scale
+    factors[1] = (m_ab + m_bb * co + m_bc * si) * scale
+    factors[2] = (m_ac + m_bc * co + m_cc * si) * scale
+
+    def change():
+        return factors[0] * comps[0] + factors[1] * comps[1] + factors[2] * comps[2]
+
+    def filter_signal(signal, out):
+        rows_to_hold(signal, halo_rows)
+        result = jnp.where(own_live, band_filter(halo_rows[...], band), 0.0)
+        for block in range(BLOCKS):
+            out[block] = result[2 * block : 2 * block + 2]
+        return result
+
+    halo_rows[...] = jnp.zeros_like(halo_rows)
+    signal_first = change()
+    filtered_first = filter_signal(signal_first, message)
+    own = halo_rows[1:9]
+    row_two[0] = (
+        jnp.where(lane == 0, total(base_own * own), 0.0)
+        + jnp.where(lane == 1, total(filtered_first * own), 0.0)
+        + jnp.where(lane == 2, over, 0.0)
+    )
+
+    pixel = rows_of((WIN, HALF)).astype(jnp.float32)
+
+    def owned_first(p, carry):
+        code = list_b[p, 0]
+        block = (code & 31) - 1
+        places, values = nine(
+            p, locate(lax.shift_right_logical(code, 5)), trig_b, live_b, lag_b
+        )
+        picked = matches(pixel, places)
+        picked_b[p] = picked
+        here = rows_of((BPD, WIN)) == block
+        for c, value in enumerate(split_product(values, picked)):
+            owned[c] += jnp.where(here, value, 0.0)
+        return carry
+
+    def three(p, where_at, trig, source):
+        f = joined(source[where_at])
+        return [f, f * joined(trig[p, 0:2, :]), f * joined(trig[p, 2:4, :])]
+
+    def owned_next(source, at):
+        def body(p, carry):
+            code = list_b[p, 0]
+            block = (code & 31) - 1
+            values = three(p, locate(lax.shift_right_logical(code, 5)), trig_b, source)
+            here = rows_of((BPD, WIN)) == block
+            for c, value in enumerate(split_product(values, picked_b[p])):
+                owned[at + c] += jnp.where(here, value, 0.0)
+            return carry
+
+        return body
+
+    def send_round(big, small, work):
+        small.start_first()
+        big.start_first()
+        work(0)
+        small.start_second()
+        big.start_second()
+        work(1)
+        small.start_small()
+        big.start_third()
+        work(2)
+        small.start_small_swap()
+        big.forward()
+        big.near()
+        big.far()
+        small.arrive()
+        big.arrive()
+
+    def sums_of(metas):
+        return jnp.sum(metas[...].reshape(DEVICES, 1, HALF), axis=0)
+
+    steps = (0, 16, 28, SLOTS)
+    send_round(
+        movers[3], movers[4],
+        lambda i: lax.fori_loop(steps[i], steps[i + 1], owned_first, 0, unroll=2),
+    )
+    sums = sums_of(meta_two)
+    product, curve = sums[:, 0:1], sums[:, 1:2]
+    over_out[...] = jnp.broadcast_to(sums[:, 2:3], (1, HALF))
+    alpha = product / curve
+    comps[0:3] = jnp.zeros((3, 8, WIN), jnp.float32)
+
+    def pair_second(p, carry):
+        code = list_a[p, 0]
+        seg = (code & 7) - 1
+        values = three(p, locate(lax.shift_right_logical(code, 3)), trig_a, all_first)
+        here = rows_of((8, WIN)) == seg
+        for c, value in enumerate(split_product(values, picked_a[p])):
+            comps[c] += jnp.where(here, value, 0.0)
+        return carry
+
+    lax.fori_loop(0, PAIRS, pair_second, 0, unroll=4)
+    filtered_second = filter_signal(signal_first - alpha * change(), message_two)
+    own = halo_rows[1:9]
+    row_two[1] = (
+        jnp.where(lane == 0, total((base_own - alpha * filtered_first) * own), 0.0)
+        + jnp.where(lane == 1, total(filtered_second * own), 0.0)
+        + jnp.where(lane == 2, total(filtered_first * own), 0.0)
+    )
+    send_round(
+        movers[5], movers[6],
+        lambda i: lax.fori_loop(steps[i], steps[i + 1], owned_next(all_first, 9), 0, unroll=4),
+    )
+    lax.fori_loop(0, SLOTS, owned_next(all_second, 12), 0, unroll=4)
+
+    sums = sums_of(meta_three)
+    product_next = sums[:, 0:1]
+    beta = product_next / product
+    curve_next = sums[:, 1:2] + 2.0 * beta * sums[:, 2:3] + beta * beta * curve
+    alpha_next = product_next / curve_next
+    m_aa, m_ab, m_ac, m_bb, m_bc, m_cc, det = adjugate(*(owned[c] for c in range(3, 9)))
+
+    def solve(r1, r2, r3):
+        return (
+            (m_aa * r1 + m_ab * r2 + m_ac * r3) / det,
+            (m_ab * r1 + m_bb * r2 + m_bc * r3) / det,
+            (m_ac * r1 + m_bc * r2 + m_cc * r3) / det,
+        )
+
+    right = [owned[c] for c in range(3)]
+    image = [owned[9 + c] for c in range(3)]
+    other = [owned[12 + c] for c in range(3)]
+    residual = [r - alpha * w for r, w in zip(right, image)]
+    start = solve(*right)
+    middle = solve(*residual)
+    final = solve(
+        *(r - alpha_next * (v + beta * w) for r, v, w in zip(residual, other, image))
+    )
+    for comp in range(3):
+        solution_out[comp] = alpha * start[comp] + alpha_next * (middle[comp] + beta * start[comp])
+        residual_out[comp] = final[comp]
+    for mover in movers:
+        mover.finish()
+    for copy in halos:
+        copy.wait_send()
+
+
 def f32(*shape):
     return jax.ShapeDtypeStruct(shape, jnp.float32)
 
@@ -539,7 +1083,7 @@
     return rows.reshape(LABELS, 2, HALF), parts.reshape(DEVICES, HALF)
 
 
-def per_device(
+def any_lengths(
     time_streams, pol_angle, offsets, block_slots, hit_ids, valid_counts, filter_taps, white_weight
 ):
     valid = valid_counts.reshape(1)
@@ -615,6 +1159,55 @@
         scratch_shapes=[pltpu.VMEM((15, BPD, WIN), jnp.float32)],
         name="last",
     )(heads, nexts, lives, lag_zero, gathered, second, third, parts_two, parts_three)
+    return tuple(answers)
+
+
+def wide_buffer(*shape):
+    return pltpu.VMEM((2, 8, 4, 4) + shape, jnp.float32)
+
+
+def room(*shape):
+    return pltpu.VMEM(shape, jnp.float32)
+
+
+def per_device(*args):
+    (
+        time_streams, pol_angle, offsets, block_slots, hit_ids, valid_counts, filter_taps,
+        white_weight,
+    ) = args
+    fast = pl.pallas_call(
+        whole_kernel,
+        out_shape=(f32(3, BPD, WIN), f32(3, BPD, WIN), f32(1, HALF)),
+        in_specs=[smem] * 4 + [vmem] * 4,
+        out_specs=(vmem,) * 3,
+        scratch_shapes=[
+            room(2, 1, HALF), room(1, WIN), room(BLOCKS, 4, HALF), room(1, HALF),
+            room(BLOCKS, 2, HALF), room(BLOCKS, 2, HALF), room(2, 1, HALF), room(BLOCKS, 2, HALF),
+            wide_buffer(BLOCKS, 4, HALF), wide_buffer(1, HALF), wide_buffer(BLOCKS, 2, HALF),
+            wide_buffer(BLOCKS, 2, HALF), wide_buffer(1, HALF), wide_buffer(BLOCKS, 2, HALF),
+            wide_buffer(1, HALF),
+            room(6, WIN, HALF),
+            pltpu.VMEM((PAIRS, WIN, WIN), jnp.bfloat16),
+            pltpu.VMEM((SLOTS, WIN, WIN), jnp.bfloat16),
+            room(PAIRS, 4, HALF), room(SLOTS, 4, HALF),
+            pltpu.SMEM((32, HALF), jnp.int32), pltpu.SMEM((SLOTS, HALF), jnp.int32),
+            room(32, HALF), room(SLOTS, HALF), room(32, HALF), room(SLOTS, HALF),
+            pltpu.VMEM((32, HALF), jnp.int32), pltpu.VMEM((SLOTS, HALF), jnp.int32),
+            room(11, 8, WIN), room(15, BPD, WIN), room(3, 8, WIN), room(16, HALF),
+            pltpu.SemaphoreType.DMA((7, 20)), pltpu.SemaphoreType.DMA((7, 20)),
+            pltpu.SemaphoreType.DMA((7,)), pltpu.SemaphoreType.DMA((2,)),
+            pltpu.SemaphoreType.DMA((2,)), pltpu.SemaphoreType.DMA((2,)),
+        ],
+        compiler_params=pltpu.CompilerParams(collective_id=3, has_side_effects=True),
+        name="whole",
+    )(
+        valid_counts.reshape(1), block_slots.reshape(BLOCKS), hit_ids.reshape(-1),
+        white_weight.reshape(1), filter_taps.reshape(1, BAND + 1), time_streams.reshape(8, HALF),
+        pol_angle.reshape(8, HALF), offsets.reshape(8, HALF),
+    )
+    answers = lax.cond(
+        fast[2][0, 0] > 0.0, lambda f, *a: any_lengths(*a), lambda f, *a: f, fast[:2], *args
+    )
     return tuple(jnp.transpose(answer, (1, 0, 2)) for answer in answers)
 
 

time: 121 us -> 81.5 us (0.67)
  Pallas kernels: 110 us -> 77.6 us
  other arithmetic: 6.33 us -> 0 us
  local copies, waits for them, and re-layouts: 2.45 us -> 1.24 us
    pallas_call x6 -> x1, Pallas kernels: 110 us -> 77.6 us  [per_device(): pl.pallas_call(whole_kernel, out_shape=(f32(3, BPD, WIN), f32(3, BPD, WIN...]
    reduce_sum x1 -> x0, other arithmetic: 3.85 us -> none  [per_device(): counts = jnp.sum(same, axis=1, dtype=jnp.int32)]
where the time goes in v2:
time: 81.5 us; the launch traced here: 81.4 us
  Pallas kernels  77.6 us (95%)
  between operations  2.5 us (3%)
  local copies, waits for them, and re-layouts  1.24 us (2%)
    pallas_call x1, Pallas kernels, per_device(): pl.pallas_call(whole_kernel, out_shape=(f32(3, BPD, WIN), f32(3, BPD, WIN...  77.6 us

profile of v2, /device:TPU:1, one launch (start us, length us, event | category | flops | bytes accessed | tf_op | source)
XLA Modules:
  0.0 81.4 jit_solution(2846942315708910161)
XLA Ops:
  1.9 77.6 %whole.1 = (f32[3,16,256]{2,1,0:T(8,128)S(1)}, f32[3,16,256]{2,1,0:T(8,128)S(1)}, f32[1,128]{1,0:T(1,128)}) custom-call(s32[1]{0:T(128)} %bitcast.27.valid, s32[4]{0:T(128)} %bitcast.50, s32[128]{0:T(128)} %bitcast.52, f32[1]{0:T(128)} %bitcast.28.white, f32[1,65]{1,0:T(1,128)} %bitcast.54, f32[8,128]{1,0:T(8,128)} %bitcast.42, f32[8,128]{1,0:T(8,128)} %bitcast.44, ...), custom_call_target="tpu_custom_call" | custom-call | tf_op jit(solution)/shard_map/whole/pallas_call | solution.py:1178
  80.1 0.6 copy.21
  80.7 0.6 copy.22
  (1 shorter events, 0.0 us)

commit v3 on v2

--- a/solution.py
+++ b/solution.py
@@ -568,7 +568,7 @@
             self.send(d - 1, self.source, own, device_at(lax.rem(z + d, 8), y, core, x))
             for d in (4, 3, 5, 2, 6, 1, 7)
         ]
-        self.keep = pltpu.make_async_copy(self.source, own, self.local_sems.at[self.number])
+        self.keep = pltpu.make_async_copy(self.source, own, self.local_sems.at[self.number, 0])
         self.keep.start()
 
     def start_second(self):
@@ -578,9 +578,6 @@
         column = self.buffer.at[self.core, :, self.a, self.b]
         self.second = [self.send(6 + d, column, column, self.major_peer(d)) for d in (2, 1, 3)]
 
-    def part(self, number, half):
-        return self.buffer.at[self.core, pl.ds(4 * half, 4), :, number]
-
     def whole(self, number):
         return self.buffer.at[self.core, :, :, number]
 
@@ -600,44 +597,79 @@
         partner = device_at(self.z, self.y, 1 - self.core, self.x)
         self.swaps = [self.pass_on(16, self.buffer.at[self.core], partner)]
 
-    def start_third(self):
-        for copy in self.second:
+    def arrive(self):
+        for copy in self.swaps:
+            copy.wait_recv()
+
+    def finish(self):
+        for copy in self.started:
+            copy.wait_send()
+
+
+class Relay(Mover):
+    ORDER = (0, 3, 1, 2)
+
+    def __init__(self, buffer, sems, number):
+        super().__init__(None, buffer, sems, number)
+        self.first, self.keep, self.sent = [], [], {}
+
+    def start_part(self, source, target, number):
+        z, y, core, x = self.z, self.y, self.core, self.x
+        self.first += [
+            self.send(number + d - 1, source, target, device_at(lax.rem(z + d, 8), y, core, x))
+            for d in (4, 3, 5, 2, 6, 1, 7)
+        ]
+        copy = pltpu.make_async_copy(source, target, self.local_sems.at[self.number, number // 7])
+        copy.start()
+        self.keep.append(copy)
+
+    def own(self):
+        return self.buffer.at[self.core, self.z, self.a, self.b]
+
+    def piece(self, k, m):
+        return self.buffer.at[
+            self.core, :, lax.rem(self.a + self.ORDER[k], 4), lax.rem(self.b + self.ORDER[m], 4)
+        ]
+
+    def pass_piece(self, number, k, m, peer):
+        self.sent[number] = self.pass_on(number, self.piece(k, m), peer)
+
+    def begin(self):
+        for copy in self.keep:
+            copy.wait()
+        for copy in self.first:
             copy.wait_recv()
         self.after, self.before = self.minor_peer(1), self.minor_peer(3)
         self.partner = device_at(self.z, self.y, 1 - self.core, self.x)
-        self.up = [self.pass_on(10, self.part(self.b, 0), self.after)]
-        self.down = [self.pass_on(12, self.part(self.b, 1), self.before)]
-        self.up.append(self.pass_on(11, self.part(self.b, 1), self.after))
-        self.down.append(self.pass_on(13, self.part(self.b, 0), self.before))
-        self.swaps = [self.pass_on(16, self.whole(self.b), self.partner)]
-
-    def forward(self):
-        left, right = lax.rem(self.b + 3, 4), lax.rem(self.b + 1, 4)
-        self.up[0].wait_recv()
-        self.up.append(self.pass_on(14, self.part(left, 0), self.after))
-        self.down[0].wait_recv()
-        self.down.append(self.pass_on(15, self.part(right, 1), self.before))
-
-    def near(self):
-        left, right = lax.rem(self.b + 3, 4), lax.rem(self.b + 1, 4)
-        self.up[1].wait_recv()
-        self.swaps.append(self.pass_on(17, self.whole(left), self.partner))
-        self.down[1].wait_recv()
-        self.swaps.append(self.pass_on(18, self.whole(right), self.partner))
-
-    def far(self):
-        far = lax.rem(self.b + 2, 4)
-        self.up[2].wait_recv()
-        self.down[2].wait_recv()
-        self.swaps.append(self.pass_on(19, self.whole(far), self.partner))
+        for d in (2, 1, 3):
+            self.sent[13 + d] = self.pass_on(13 + d, self.piece(0, 0), self.major_peer(d))
+        self.spread(0)
+
+    def spread(self, k):
+        if k:
+            self.sent[(None, 14, 16, 15)[k]].wait_recv()
+        self.pass_piece(17 + k, k, 0, self.after)
+        self.pass_piece(21 + k, k, 0, self.before)
+        self.pass_piece(29 + 4 * k, k, 0, self.partner)
+
+    def hop(self, k):
+        self.sent[17 + k].wait_recv()
+        if k in (0, 2):
+            self.pass_piece(25 + k, k, 1, self.after)
+        self.pass_piece(30 + 4 * k, k, 1, self.partner)
+        self.sent[21 + k].wait_recv()
+        if k in (1, 3):
+            self.pass_piece(25 + k, k, 2, self.before)
+        self.pass_piece(31 + 4 * k, k, 2, self.partner)
+
+    def last(self, k):
+        self.sent[25 + k].wait_recv()
+        self.pass_piece(32 + 4 * k, k, 3, self.partner)
 
     def arrive(self):
-        for copy in self.swaps:
-            copy.wait_recv()
-
-    def finish(self):
-        for copy in self.started:
-            copy.wait_send()
+        for k in range(4):
+            for m in range(4):
+                self.sent[29 + 4 * k + m].wait_recv()
 
 
 def locate(label):
@@ -753,10 +785,10 @@
 def whole_kernel(
     valid, slots, hits, white, taps, stream, angle, offset,
     solution_out, residual_out, over_out,
-    hold, taps_row, fixed, meta, base, message, row_two, message_two,
-    all_fixed, all_meta, all_base, all_first, meta_two, all_second, meta_three,
+    hold, hold_fixed, taps_row, fixed, meta, base, message, row_two, message_two,
+    all_fixed, all_meta, all_first, meta_two, all_second, meta_three,
     columns, picked_a, picked_b, trig_a, trig_b, list_a, list_b, live_a, live_b, lag_a, lag_b,
-    near_a, near_b, comps, owned, factors, halo_rows,
+    near_a, near_b, comps, owned, factors, halo_rows, inverse,
     send_sems, recv_sems, local_sems, halo_send, halo_recv, list_sems,
 ):
     z, y, core, x = grid_place()
@@ -773,25 +805,16 @@
 
     place_of = offset[...].astype(jnp.float32)
     for block in range(BLOCKS):
-        fixed[block, 0:2, :] = angle[2 * block : 2 * block + 2]
-        fixed[block, 2:4, :] = place_of[2 * block : 2 * block + 2]
+        fixed[block, 0] = angle[2 * block : 2 * block + 2]
+        fixed[block, 1] = place_of[2 * block : 2 * block + 2]
     taps_row[...] = jnp.zeros_like(taps_row)
     taps_row[:, : BAND + 1] = taps[...]
-    spread = jnp.broadcast_to(taps_row[...], (WIN, WIN))
-    shifted = pltpu.roll(spread, HALF, 1, stride=1, stride_axis=0)
-    lag_row = lax.dot_general(
-        spread[:8], shifted, NT, precision=HIGHEST, preferred_element_type=jnp.float32
-    )
-    lag_row = lag_row + jnp.where(lanes((8, WIN)) == HALF, white[0], 0.0)
-    band = pltpu.roll(
-        jnp.broadcast_to(lag_row[0:1], (WIN, WIN)), WIN - HALF - BAND, 1, stride=1, stride_axis=0
-    )[:, :HALF]
-    lag_zero = lag_row[0:1, HALF : HALF + 1]
-    remaining = valid[0] - tm * SPAN
+    lag_zero = jnp.sum(taps_row[...] * taps_row[...], axis=1, keepdims=True) + white[0, 0]
+    remaining = valid[0, 0] - tm * SPAN
     lane = lanes((1, HALF))
     header = jnp.where(lane == 8, jnp.broadcast_to(lag_zero, (1, HALF)), 0.0)
     for block in range(BLOCKS):
-        found = hits[slots[block]].astype(jnp.float32)
+        found = hits[0, slots[0, block]].astype(jnp.float32)
         count = jnp.clip(remaining - block * WIN, 0, WIN).astype(jnp.float32)
         header = jnp.where(lane == block, found, header)
         header = jnp.where(lane == 4 + block, count, header)
@@ -801,51 +824,93 @@
     pl.semaphore_wait(barrier, len(peers))
     halos = [
         pltpu.make_async_remote_copy(
-            src_ref=stream.at[pl.ds(at, 1)],
-            dst_ref=hold.at[i],
+            src_ref=source,
+            dst_ref=target,
             send_sem=halo_send.at[i],
             recv_sem=halo_recv.at[i],
             device_id=device_at(z, y, core, lax.rem(x + step, 4)),
             device_id_type=MESH,
         )
-        for i, (at, step) in enumerate(((7, 1), (0, 3)))
+        for i, (source, target, step) in enumerate(
+            (
+                (stream.at[pl.ds(7, 1)], hold.at[0], 1),
+                (stream.at[pl.ds(0, 1)], hold.at[1], 3),
+                (fixed.at[BLOCKS - 1], hold_fixed.at[0], 1),
+                (fixed.at[0], hold_fixed.at[1], 3),
+            )
+        )
     ]
     for copy in halos:
         copy.start()
     sems = (send_sems, recv_sems, local_sems)
-    movers = [
-        Mover(fixed, all_fixed, sems, 0),
-        Mover(meta, all_meta, sems, 1),
-        Mover(base, all_base, sems, 2),
-        Mover(message, all_first, sems, 3),
-        Mover(row_two.at[0], meta_two, sems, 4),
-        Mover(message_two, all_second, sems, 5),
-        Mover(row_two.at[1], meta_three, sems, 6),
+    smalls = [
+        Mover(meta, all_meta, sems, 0),
+        Mover(row_two.at[0], meta_two, sems, 1),
+        Mover(row_two.at[1], meta_three, sems, 2),
     ]
-    big, small, mid = movers[:3]
+    relays = [
+        Relay(all_fixed, sems, 3),
+        Relay(all_first, sems, 4),
+        Relay(all_second, sems, 5),
+    ]
+    big, small = relays[0], smalls[0]
     small.start_first()
-    big.start_first()
-
-    for copy in halos:
+    big.start_part(fixed, big.own().at[:, pl.ds(0, 2)], 0)
+
+    spread = jnp.broadcast_to(taps_row[...], (WIN, WIN))
+    shifted = pltpu.roll(spread, HALF, 1, stride=1, stride_axis=0)
+    lag_row = lax.dot_general(
+        spread[:8], shifted, NT, precision=HIGHEST, preferred_element_type=jnp.float32
+    )
+    lag_row = lag_row + jnp.where(lanes((8, WIN)) == HALF, white[0, 0], 0.0)
+    band = pltpu.roll(
+        jnp.broadcast_to(lag_row[0:1], (WIN, WIN)), WIN - HALF - BAND, 1, stride=1, stride_axis=0
+    )[:, :HALF]
+    for copy in halos[:2]:
         copy.wait_recv()
     extended = jnp.concatenate(
         [hold[0], stream[...], hold[1], jnp.zeros((6, HALF), jnp.float32)], axis=0
     )
     place = (rows_of((16, HALF)) - 1) * HALF + lanes((16, HALF))
     extended = jnp.where((place < remaining) & (place + tm * SPAN >= 0), extended, 0.0)
-    filtered = jnp.where(own_live, band_filter(extended, band), 0.0)
-    base_own = filtered
+    base_own = jnp.where(own_live, band_filter(extended, band), 0.0)
     for block in range(BLOCKS):
-        base[block] = filtered[2 * block : 2 * block + 2]
-    mid.start_first()
+        base[block, 0] = base_own[2 * block : 2 * block + 2]
+    big.start_part(base, big.own().at[:, pl.ds(2, 1)], 7)
+
+    comps[...] = jnp.zeros_like(comps)
+    owned[...] = jnp.zeros_like(owned)
+    halo_rows[...] = jnp.zeros_like(halo_rows)
+    for copy in halos[2:]:
+        copy.wait_recv()
+    segments = (
+        [(hold_fixed[0, 0], hold_fixed[0, 1])]
+        + [(fixed[block, 0], fixed[block, 1]) for block in range(BLOCKS)]
+        + [(hold_fixed[1, 0], hold_fixed[1, 1])]
+    )
+    for seg, (turn, _) in enumerate(segments):
+        comps[9, seg : seg + 1, :] = joined(turn)
+    rows = [places for _, places in segments]
+    turned = jnp.concatenate(
+        rows + [jnp.zeros((HALF - 12, HALF), jnp.float32)], axis=0
+    ).T
+    for seg in range(6):
+        for half in range(2):
+            at = 2 * seg + half
+            columns[seg, HALF * half : HALF * half + HALF, :] = jnp.broadcast_to(
+                turned[:, at : at + 1], (HALF, HALF)
+            )
+    turn = 2.0 * comps[9]
+    comps[9] = jnp.cos(turn)
+    comps[10] = jnp.sin(turn)
 
     small.start_second()
-    big.start_second()
-    mid.start_second()
+    big.begin()
     small.start_small()
-    big.start_third()
-    mid.start_third()
+    big.spread(1)
+    big.spread(2)
     small.start_small_swap()
+    big.hop(0)
     small.arrive()
     over = make_lists(all_meta, near_a, near_b, live_a, live_b, lag_a, lag_b)
     copies = [
@@ -854,52 +919,38 @@
     ]
     for copy in copies:
         copy.start()
-    big.forward()
-    mid.forward()
-    big.near()
-    mid.near()
-    big.far()
-    mid.far()
+
+    def wind_up(big):
+        big.spread(3)
+        big.hop(1)
+        big.hop(2)
+        big.last(0)
+        big.last(1)
+        big.last(2)
+        big.hop(3)
+        big.last(3)
+
+    wind_up(big)
     for copy in copies:
         copy.wait()
-    comps[...] = jnp.zeros_like(comps)
-    owned[...] = jnp.zeros_like(owned)
     big.arrive()
-    mid.arrive()
-
-    labels, usable = own_labels()
-    rows = []
-    for seg in range(6):
-        tile = all_fixed[locate(labels[seg])]
-        rows.append(tile[2:4])
-        turn = 2.0 * tile[0:2]
-        comps[9, seg : seg + 1, :] = joined(jnp.cos(turn))
-        comps[10, seg : seg + 1, :] = joined(jnp.sin(turn))
-    rows.append(jnp.zeros((HALF - 12, HALF), jnp.float32))
-    turned = jnp.concatenate(rows, axis=0).T
-    for seg in range(6):
-        for half in range(2):
-            at = 2 * seg + half
-            columns[seg, HALF * half : HALF * half + HALF, :] = jnp.broadcast_to(
-                turned[:, at : at + 1], (HALF, HALF)
-            )
+
     wide_lane = lanes((1, WIN)).astype(jnp.float32)
 
     def doubled(row):
         return jnp.concatenate([row, row], axis=1)
 
     def nine(p, where_at, trig, live, lag):
-        tile = all_fixed[where_at]
-        turn = 2.0 * tile[0:2]
+        turn = 2.0 * all_fixed[where_at + (0,)]
         co2, si2 = jnp.cos(turn), jnp.sin(turn)
         trig[p, 0:2, :] = co2
         trig[p, 2:4, :] = si2
         co, si = joined(co2), joined(si2)
-        f = joined(all_base[where_at])
+        f = joined(all_fixed[where_at + (2,)])
         weight = jnp.where(
             wide_lane < doubled(live[pl.ds(p, 1), :]), doubled(lag[pl.ds(p, 1), :]), 0.0
         )
-        return tile[2:4], [f, f * co, f * si] + weight_rows(weight, co, si)
+        return all_fixed[where_at + (1,)], [f, f * co, f * si] + weight_rows(weight, co, si)
 
     def pair_first(p, carry):
         code = list_a[p, 0]
@@ -919,7 +970,7 @@
     co, si = comps[9], comps[10]
     seg_row = rows_of((8, WIN))
     time = tm * SPAN + (seg_row - 1) * WIN + lanes((8, WIN))
-    live = (time >= 0) & (time < valid[0]) & (seg_row < 6)
+    live = (time >= 0) & (time < valid[0, 0]) & (seg_row < 6)
     scale = jnp.where(live, 1.0, 0.0) / det
     factors[0] = (m_aa + m_ab * co + m_ac * si) * scale
     factors[1] = (m_ab + m_bb * co + m_bc * si) * scale
@@ -935,7 +986,6 @@
             out[block] = result[2 * block : 2 * block + 2]
         return result
 
-    halo_rows[...] = jnp.zeros_like(halo_rows)
     signal_first = change()
     filtered_first = filter_signal(signal_first, message)
     own = halo_rows[1:9]
@@ -976,32 +1026,30 @@
 
         return body
 
-    def send_round(big, small, work):
-        small.start_first()
-        big.start_first()
-        work(0)
-        small.start_second()
-        big.start_second()
-        work(1)
-        small.start_small()
-        big.start_third()
-        work(2)
-        small.start_small_swap()
-        big.forward()
-        big.near()
-        big.far()
-        small.arrive()
-        big.arrive()
-
     def sums_of(metas):
         return jnp.sum(metas[...].reshape(DEVICES, 1, HALF), axis=0)
 
-    steps = (0, 16, 28, SLOTS)
-    send_round(
-        movers[3], movers[4],
-        lambda i: lax.fori_loop(steps[i], steps[i + 1], owned_first, 0, unroll=2),
-    )
-    sums = sums_of(meta_two)
+    def send_round(big, source, small, metas, work):
+        big.start_part(source, big.own(), 0)
+        small.start_first()
+        work()
+        big.begin()
+        small.start_second()
+        big.spread(1)
+        big.spread(2)
+        small.start_small()
+        big.hop(0)
+        small.start_small_swap()
+        wind_up(big)
+        small.arrive()
+        sums = sums_of(metas)
+        big.arrive()
+        return sums
+
+    def owned_weights():
+        lax.fori_loop(0, SLOTS, owned_first, 0, unroll=2)
+
+    sums = send_round(relays[1], message, smalls[1], meta_two, owned_weights)
     product, curve = sums[:, 0:1], sums[:, 1:2]
     over_out[...] = jnp.broadcast_to(sums[:, 2:3], (1, HALF))
     alpha = product / curve
@@ -1024,39 +1072,43 @@
         + jnp.where(lane == 1, total(filtered_second * own), 0.0)
         + jnp.where(lane == 2, total(filtered_first * own), 0.0)
     )
-    send_round(
-        movers[5], movers[6],
-        lambda i: lax.fori_loop(steps[i], steps[i + 1], owned_next(all_first, 9), 0, unroll=4),
-    )
-    lax.fori_loop(0, SLOTS, owned_next(all_second, 12), 0, unroll=4)
-
-    sums = sums_of(meta_three)
+
+    def solve(r1, r2, r3):
+        i_aa, i_ab, i_ac, i_bb, i_bc, i_cc = (inverse[c] for c in range(6))
+        return (
+            i_aa * r1 + i_ab * r2 + i_ac * r3,
+            i_ab * r1 + i_bb * r2 + i_bc * r3,
+            i_ac * r1 + i_bc * r2 + i_cc * r3,
+        )
+
+    def owned_images():
+        lax.fori_loop(0, SLOTS, owned_next(all_first, 9), 0, unroll=4)
+        *minors, det = adjugate(*(owned[c] for c in range(3, 9)))
+        scale = 1.0 / det
+        for c, minor in enumerate(minors):
+            inverse[c] = minor * scale
+        start = solve(*(owned[c] for c in range(3)))
+        for c in range(3):
+            owned[c] = owned[c] - alpha * owned[9 + c]
+        middle = solve(*(owned[c] for c in range(3)))
+        for c in range(3):
+            owned[3 + c] = start[c]
+            owned[6 + c] = middle[c]
+
+    sums = send_round(relays[2], message_two, smalls[2], meta_three, owned_images)
     product_next = sums[:, 0:1]
     beta = product_next / product
     curve_next = sums[:, 1:2] + 2.0 * beta * sums[:, 2:3] + beta * beta * curve
     alpha_next = product_next / curve_next
-    m_aa, m_ab, m_ac, m_bb, m_bc, m_cc, det = adjugate(*(owned[c] for c in range(3, 9)))
-
-    def solve(r1, r2, r3):
-        return (
-            (m_aa * r1 + m_ab * r2 + m_ac * r3) / det,
-            (m_ab * r1 + m_bb * r2 + m_bc * r3) / det,
-            (m_ac * r1 + m_bc * r2 + m_cc * r3) / det,
-        )
-
-    right = [owned[c] for c in range(3)]
-    image = [owned[9 + c] for c in range(3)]
-    other = [owned[12 + c] for c in range(3)]
-    residual = [r - alpha * w for r, w in zip(right, image)]
-    start = solve(*right)
-    middle = solve(*residual)
-    final = solve(
-        *(r - alpha_next * (v + beta * w) for r, v, w in zip(residual, other, image))
-    )
-    for comp in range(3):
-        solution_out[comp] = alpha * start[comp] + alpha_next * (middle[comp] + beta * start[comp])
-        residual_out[comp] = final[comp]
-    for mover in movers:
+    for c in range(3):
+        start = owned[3 + c]
+        solution_out[c] = alpha * start + alpha_next * (owned[6 + c] + beta * start)
+        owned[c] = owned[c] - alpha_next * beta * owned[9 + c]
+    lax.fori_loop(0, SLOTS, owned_next(all_second, 12), 0, unroll=4)
+    final = solve(*(owned[c] - alpha_next * owned[12 + c] for c in range(3)))
+    for c in range(3):
+        residual_out[c] = final[c]
+    for mover in smalls + relays:
         mover.finish()
     for copy in halos:
         copy.wait_send()
@@ -1181,11 +1233,11 @@
         in_specs=[smem] * 4 + [vmem] * 4,
         out_specs=(vmem,) * 3,
         scratch_shapes=[
-            room(2, 1, HALF), room(1, WIN), room(BLOCKS, 4, HALF), room(1, HALF),
-            room(BLOCKS, 2, HALF), room(BLOCKS, 2, HALF), room(2, 1, HALF), room(BLOCKS, 2, HALF),
-            wide_buffer(BLOCKS, 4, HALF), wide_buffer(1, HALF), wide_buffer(BLOCKS, 2, HALF),
-            wide_buffer(BLOCKS, 2, HALF), wide_buffer(1, HALF), wide_buffer(BLOCKS, 2, HALF),
-            wide_buffer(1, HALF),
+            room(2, 1, HALF), room(2, 2, 2, HALF), room(1, WIN), room(BLOCKS, 2, 2, HALF),
+            room(1, HALF), room(BLOCKS, 1, 2, HALF), room(BLOCKS, 2, HALF), room(2, 1, HALF),
+            room(BLOCKS, 2, HALF),
+            wide_buffer(BLOCKS, 3, 2, HALF), wide_buffer(1, HALF), wide_buffer(BLOCKS, 2, HALF),
+            wide_buffer(1, HALF), wide_buffer(BLOCKS, 2, HALF), wide_buffer(1, HALF),
             room(6, WIN, HALF),
             pltpu.VMEM((PAIRS, WIN, WIN), jnp.bfloat16),
             pltpu.VMEM((SLOTS, WIN, WIN), jnp.bfloat16),
@@ -1194,15 +1246,16 @@
             room(32, HALF), room(SLOTS, HALF), room(32, HALF), room(SLOTS, HALF),
             pltpu.VMEM((32, HALF), jnp.int32), pltpu.VMEM((SLOTS, HALF), jnp.int32),
             room(11, 8, WIN), room(15, BPD, WIN), room(3, 8, WIN), room(16, HALF),
-            pltpu.SemaphoreType.DMA((7, 20)), pltpu.SemaphoreType.DMA((7, 20)),
-            pltpu.SemaphoreType.DMA((7,)), pltpu.SemaphoreType.DMA((2,)),
-            pltpu.SemaphoreType.DMA((2,)), pltpu.SemaphoreType.DMA((2,)),
+            room(6, BPD, WIN),
+            pltpu.SemaphoreType.DMA((6, 45)), pltpu.SemaphoreType.DMA((6, 45)),
+            pltpu.SemaphoreType.DMA((6, 2)), pltpu.SemaphoreType.DMA((4,)),
+            pltpu.SemaphoreType.DMA((4,)), pltpu.SemaphoreType.DMA((2,)),
         ],
         compiler_params=pltpu.CompilerParams(collective_id=3, has_side_effects=True),
         name="whole",
     )(
-        valid_counts.reshape(1), block_slots.reshape(BLOCKS), hit_ids.reshape(-1),
-        white_weight.reshape(1), filter_taps.reshape(1, BAND + 1), time_streams.reshape(8, HALF),
+        valid_counts, block_slots.reshape(1, BLOCKS), hit_ids, white_weight,
+        filter_taps.reshape(1, BAND + 1), time_streams.reshape(8, HALF),
         pol_angle.reshape(8, HALF), offsets.reshape(8, HALF),
     )
     answers = lax.cond(

time: 81.5 us -> 97.5 us (1.20)
  Pallas kernels: 77.6 us -> 93.6 us
    pallas_call x1, Pallas kernels: 77.6 us -> 93.6 us  [per_device(): pl.pallas_call(whole_kernel, out_shape=(f32(3, BPD, WIN), f32(3, BPD, WIN...]
where the time goes in v3:
time: 97.5 us; the launch traced here: 97.3 us
  Pallas kernels  93.6 us (96%)
  between operations  2.5 us (3%)
  local copies, waits for them, and re-layouts  1.24 us (1%)
    pallas_call x1, Pallas kernels, per_device(): pl.pallas_call(whole_kernel, out_shape=(f32(3, BPD, WIN), f32(3, BPD, WIN...  93.6 us

profile of v3, /device:TPU:1, one launch (start us, length us, event | category | flops | bytes accessed | tf_op | source)
XLA Modules:
  0.0 97.3 jit_solution(4491617490035571809)
XLA Ops:
  1.9 93.6 %whole.1 = (f32[3,16,256]{2,1,0:T(8,128)S(1)}, f32[3,16,256]{2,1,0:T(8,128)S(1)}, f32[1,128]{1,0:T(1,128)}) custom-call(s32[1,1]{1,0:T(1,128)S(6)} %copy.19.valid, s32[1,4]{1,0:T(1,128)} %bitcast.45, s32[1,128]{1,0:T(1,128)} %hits.1, f32[1,1]{1,0:T(1,128)S(6)} %copy.20.white, f32[1,65]{1,0:T(1,128)} %bitcast.48, f32[8,128]{1,0:T(8,128)} %bitcast.37, ...), custom_call_target="tpu_custom_call" | custom-call | tf_op jit(solution)/shard_map/whole/pallas_call | solution.py:1230
  96.1 0.6 copy.21
  96.7 0.6 copy.22
  (1 shorter events, 0.0 us)

commit v4 on v1

--- a/solution.py
+++ b/solution.py
@@ -14,6 +14,8 @@
 SPAN = 1024
 BLOCKS = 4
 DEVICES = 256
+PAIRS = 28
+SLOTS = 20
 LABELS = DEVICES * BLOCKS
 
 HIGHEST = lax.Precision.HIGHEST
@@ -518,6 +520,617 @@
         residual_out[comp] = final[comp]
 
 
+class Mover:
+    def __init__(self, source, buffer, sems, number):
+        self.source, self.buffer = source, buffer
+        self.send_sems, self.recv_sems, self.local_sems = sems
+        self.number = number
+        self.z, self.y, self.core, self.x = grid_place()
+        self.started = []
+
+    def send(self, number, source, target, peer):
+        copy = pltpu.make_async_remote_copy(
+            src_ref=source,
+            dst_ref=target,
+            send_sem=self.send_sems.at[self.number, number],
+            recv_sem=self.recv_sems.at[self.number, number],
+            device_id=peer,
+            device_id_type=MESH,
+        )
+        copy.start()
+        self.started.append(copy)
+        return copy
+
+    def start_first(self):
+        z, y, core, x = self.z, self.y, self.core, self.x
+        own = self.buffer.at[z, y]
+        self.first = [
+            self.send(d - 1, self.source, own, device_at(lax.rem(z + d, 8), y, core, x))
+            for d in (4, 3, 5, 2, 6, 1, 7)
+        ]
+        self.keep = pltpu.make_async_copy(self.source, own, self.local_sems.at[self.number])
+        self.keep.start()
+
+    def start_second(self):
+        self.keep.wait()
+        for copy in self.first:
+            copy.wait_recv()
+        column = self.buffer.at[:, self.y]
+        self.second = [
+            self.send(
+                6 + d, column, column,
+                device_at(self.z, lax.rem(self.y + d, 4), self.core, self.x),
+            )
+            for d in (2, 1, 3)
+        ]
+
+    def arrive(self):
+        for copy in self.second:
+            copy.wait_recv()
+
+    def finish(self):
+        for copy in self.started:
+            copy.wait_send()
+
+
+class Group:
+    def __init__(self, send_sems, recv_sems):
+        self.send_sems, self.recv_sems = send_sems, recv_sems
+        self.z, self.y, self.core, self.x = grid_place()
+        self.me = self.x * 2 + self.core
+        self.started = []
+
+    def send(self, number, k, source, target, peer):
+        copy = pltpu.make_async_remote_copy(
+            src_ref=source,
+            dst_ref=target,
+            send_sem=self.send_sems.at[number, k],
+            recv_sem=self.recv_sems.at[number, k],
+            device_id=peer,
+            device_id_type=MESH,
+        )
+        copy.start()
+        self.started.append(copy)
+        return copy
+
+    def to_all(self, number, source_of, target):
+        copies = []
+        for k in (4, 5, 2, 3, 6, 7, 1):
+            x = lax.rem(self.x + k // 2, 4)
+            core = lax.rem(self.core + k % 2, 2)
+            copies.append(
+                self.send(
+                    number, k, source_of(x * 2 + core), target, device_at(self.z, self.y, core, x)
+                )
+            )
+        return copies
+
+    def to_partner(self, number, source, target):
+        return [
+            self.send(number, 0, source, target, device_at(self.z, self.y, 1 - self.core, self.x))
+        ]
+
+    def along(self, number, ref):
+        return [
+            self.send(
+                number, d, ref, ref, device_at(self.z, self.y, self.core, lax.rem(self.x + d, 4))
+            )
+            for d in (2, 1, 3)
+        ]
+
+    def finish(self):
+        for copy in self.started:
+            copy.wait_send()
+
+
+def landed(copies):
+    for copy in copies:
+        copy.wait_recv()
+
+
+def locate(label):
+    return (
+        lax.shift_right_logical(label, 2) & 7,
+        label & 3,
+        lax.shift_right_logical(label, 5) & 3,
+    )
+
+
+def joined(tile):
+    return jnp.concatenate([tile[0:1], tile[1:2]], axis=1)
+
+
+def split_product(rows, picked):
+    count = len(rows)
+    values = jnp.concatenate(rows, axis=0)
+    high = values.astype(jnp.bfloat16).astype(jnp.float32)
+    rest = values - high
+    middle = rest.astype(jnp.bfloat16).astype(jnp.float32)
+    low = rest - middle
+    pad = -3 * count % 16
+    stack = [high, middle, low]
+    if pad:
+        stack.append(jnp.zeros((pad, WIN), jnp.float32))
+    left = jnp.concatenate(stack, axis=0).astype(jnp.bfloat16)
+    out = lax.dot_general(left, picked, NT, preferred_element_type=jnp.float32)
+    return [
+        out[c : c + 1] + out[count + c : count + c + 1] + out[2 * count + c : 2 * count + c + 1]
+        for c in range(count)
+    ]
+
+
+def matches(column, places):
+    low = jnp.where(column == places[0:1], 1.0, 0.0)
+    high = jnp.where(column == places[1:2], 1.0, 0.0)
+    return jnp.concatenate([low, high], axis=1).astype(jnp.bfloat16)
+
+
+def make_lists(metas, group_meta, list_a, list_b, live_a, live_b, lag_a, lag_b):
+    z, y, core, x = grid_place()
+    table = jnp.concatenate(
+        [metas[...].reshape(32, HALF), jnp.zeros((HALF - 32, HALF), jnp.float32)], axis=0
+    ).T
+
+    def lane_row(rows):
+        out = rows[0]
+        for j in range(1, 4):
+            out = out + pltpu.roll(rows[j], 32 * j, 1)
+        return out
+
+    blocks = lane_row([table[j : j + 1] for j in range(4)])
+    lives = lane_row([table[4 + j : 5 + j] for j in range(4)])
+    lags = lane_row([table[8:9]] * 4)
+    label = lanes((1, HALF)).astype(jnp.float32)
+    none = jnp.full((1, 1), -5.0, jnp.float32)
+    wanted = []
+    for t in range(8):
+        wanted.append(group_meta[t - 2][:, 3:4] if t >= 2 else none)
+        wanted += [group_meta[t][:, j : j + 1] for j in range(BLOCKS)]
+        wanted.append(group_meta[t + 2][:, 0:1] if t < 6 else none)
+    wanted = jnp.concatenate(wanted, axis=0)
+    base = ((z * 4 + y) * 2 * BPD).astype(jnp.float32)
+    mask = jnp.concatenate(
+        [
+            jnp.where(wanted == blocks, 1.0, 0.0),
+            jnp.where((blocks >= base) & (blocks < base + 2 * BPD), 1.0, 0.0),
+            jnp.zeros((15, HALF), jnp.float32),
+        ],
+        axis=0,
+    )
+    ahead = jnp.where(rows_of((HALF, HALF)) < lanes((HALF, HALF)), 1.0, 0.0)
+    within = jnp.dot(mask, ahead, precision=HIGHEST, preferred_element_type=jnp.float32)
+    totals = jnp.broadcast_to(jnp.sum(mask, axis=1, keepdims=True), (64, HALF))
+    above = jnp.where(
+        (rows_of((64, 64)) > lanes((64, 64))) & ((rows_of((64, 64)) >= 48) == (lanes((64, 64)) >= 48)),
+        1.0, 0.0,
+    )
+    rank = within + jnp.dot(above, totals, precision=HIGHEST, preferred_element_type=jnp.float32)
+    rank = jnp.where(mask > 0.0, rank, -1.0)
+    count_a = jnp.sum(totals[0:48, 0:1], axis=0, keepdims=True)
+    count_b = totals[48:49, 0:1]
+    over = jnp.where((count_a > PAIRS) | (count_b > SLOTS), 1.0, 0.0)
+
+    def spread(values):
+        return jnp.broadcast_to(jnp.sum(values, axis=1, keepdims=True), values.shape)
+
+    def store(code, list_ref, live_ref, lag_ref):
+        list_ref[...] = spread(code).astype(jnp.int32)
+        live_ref[...] = spread(jnp.where(code > 0.0, lives, 0.0))
+        lag_ref[...] = spread(jnp.where(code > 0.0, lags, 0.0))
+
+    slot = rows_of((32, HALF)).astype(jnp.float32)
+    code = jnp.zeros((32, HALF), jnp.float32)
+    for r in range(48):
+        row = 5 * (r // 6) + (4, 0, 1, 2, 3, 4)[r % 6]
+        code += jnp.where(slot == rank[r : r + 1], label * 4096.0 + ((row + 1) * 64.0 + r + 1.0), 0.0)
+    store(code, list_a, live_a, lag_a)
+    slot = rows_of((24, HALF)).astype(jnp.float32)
+    code = jnp.where(slot == rank[48:49], label * 64.0 + (blocks - base + 1.0), 0.0)
+    store(code, list_b, live_b, lag_b)
+    return over
+
+
+def placing(codes, shift, count):
+    row = (lax.shift_right_logical(codes, shift) & 63) - 1
+    here = jnp.where(row == lanes(codes.shape), 1.0, 0.0)
+    size = codes.shape[0]
+    square = jnp.concatenate([here, jnp.zeros((HALF - size, HALF), jnp.float32)], axis=0).T
+    return square[0:count, 0:size]
+
+
+def whole_kernel(
+    valid, slots, hits, white, taps, stream, angle, offset,
+    solution_out, residual_out, over_out,
+    hold, taps_row, fixed, meta, base, message, row_two, message_two,
+    all_fixed, all_base, all_meta, all_first, meta_two, all_second, meta_three,
+    group_fixed, group_meta, sums_out, sums_in, next_out, next_in, last_row, group_row,
+    columns, picked_a, picked_b, trig_a, trig_b, list_a, list_b, live_a, live_b, lag_a, lag_b,
+    near_a, near_b, result_a, result_b, comps, factors, halo_rows,
+    own_part, partner_part, x_part, owned, inverse,
+    send_sems, recv_sems, local_sems, group_send, group_recv, halo_send, halo_recv, list_sems,
+):
+    z, y, core, x = grid_place()
+    tm = x
+    barrier = pltpu.get_barrier_semaphore()
+    peers = [device_at(lax.rem(z + d, 8), y, core, x) for d in range(1, 8)] + [
+        device_at(z, lax.rem(y + d, 4), core, x) for d in range(1, 4)
+    ]
+    for k in range(1, 8):
+        peers.append(device_at(z, y, lax.rem(core + k % 2, 2), lax.rem(x + k // 2, 4)))
+    for peer in peers:
+        pl.semaphore_signal(barrier, inc=1, device_id=peer, device_id_type=MESH)
+
+    place_of = offset[...].astype(jnp.float32)
+    for block in range(BLOCKS):
+        fixed[block, 0] = angle[2 * block : 2 * block + 2]
+        fixed[block, 1] = place_of[2 * block : 2 * block + 2]
+    taps_row[...] = jnp.zeros_like(taps_row)
+    taps_row[:, : BAND + 1] = taps[...]
+    lag_zero = jnp.sum(taps_row[...] * taps_row[...], axis=1, keepdims=True) + white[0, 0]
+    remaining = valid[0, 0] - tm * SPAN
+    lane = lanes((1, HALF))
+    header = jnp.where(lane == 8, jnp.broadcast_to(lag_zero, (1, HALF)), 0.0)
+    for block in range(BLOCKS):
+        found = hits[0, slots[0, block]].astype(jnp.float32)
+        count = jnp.clip(remaining - block * WIN, 0, WIN).astype(jnp.float32)
+        header = jnp.where(lane == block, found, header)
+        header = jnp.where(lane == 4 + block, count, header)
+    meta[...] = header
+    own_live = rows_of((8, HALF)) * HALF + lanes((8, HALF)) < remaining
+
+    pl.semaphore_wait(barrier, len(peers))
+    halos = [
+        pltpu.make_async_remote_copy(
+            src_ref=source,
+            dst_ref=target,
+            send_sem=halo_send.at[i],
+            recv_sem=halo_recv.at[i],
+            device_id=device_at(z, y, core, lax.rem(x + step, 4)),
+            device_id_type=MESH,
+        )
+        for i, (source, target, step) in enumerate(
+            (
+                (stream.at[pl.ds(7, 1)], hold.at[0], 1),
+                (stream.at[pl.ds(0, 1)], hold.at[1], 3),
+            )
+        )
+    ]
+    for copy in halos:
+        copy.start()
+    sems = (send_sems, recv_sems, local_sems)
+    smalls = [
+        Mover(meta, all_meta, sems, 0),
+        Mover(row_two.at[0], meta_two, sems, 1),
+        Mover(row_two.at[1], meta_three, sems, 2),
+    ]
+    relays = [
+        Mover(fixed, all_fixed, sems, 3),
+        Mover(message, all_first, sems, 4),
+        Mover(message_two, all_second, sems, 5),
+        Mover(base, all_base, sems, 6),
+    ]
+    group = Group(group_send, group_recv)
+    me = group.me
+    big, small, mid = relays[0], smalls[0], relays[3]
+    small.start_first()
+    big.start_first()
+    places_in = group.to_all(0, lambda t: fixed, group_fixed.at[me])
+    blocks_in = group.to_all(1, lambda t: meta, group_meta.at[me])
+    group_fixed[me] = fixed[...]
+    group_meta[me] = meta[...]
+
+    spread = jnp.broadcast_to(taps_row[...], (WIN, WIN))
+    shifted = pltpu.roll(spread, HALF, 1, stride=1, stride_axis=0)
+    lag_row = lax.dot_general(
+        spread[:8], shifted, NT, precision=HIGHEST, preferred_element_type=jnp.float32
+    )
+    lag_row = lag_row + jnp.where(lanes((8, WIN)) == HALF, white[0, 0], 0.0)
+    band = pltpu.roll(
+        jnp.broadcast_to(lag_row[0:1], (WIN, WIN)), WIN - HALF - BAND, 1, stride=1, stride_axis=0
+    )[:, :HALF]
+    landed(halos)
+    extended = jnp.concatenate(
+        [hold[0], stream[...], hold[1], jnp.zeros((6, HALF), jnp.float32)], axis=0
+    )
+    place = (rows_of((16, HALF)) - 1) * HALF + lanes((16, HALF))
+    extended = jnp.where((place < remaining) & (place + tm * SPAN >= 0), extended, 0.0)
+    base_own = jnp.where(own_live, band_filter(extended, band), 0.0)
+    for block in range(BLOCKS):
+        base[block] = base_own[2 * block : 2 * block + 2]
+    mid.start_first()
+
+    comps[...] = jnp.zeros_like(comps)
+    halo_rows[...] = jnp.zeros_like(halo_rows)
+    result_a[...] = jnp.zeros_like(result_a)
+    result_b[...] = jnp.zeros_like(result_b)
+    landed(places_in)
+    landed(blocks_in)
+    for block in range(BLOCKS):
+        comps[9, block : block + 1, :] = joined(fixed[block, 0])
+    right = group_fixed[jnp.minimum(x + 1, 3) * 2 + core, 0, 0]
+    left = group_fixed[jnp.maximum(x - 1, 0) * 2 + core, BLOCKS - 1, 0]
+    comps[9, 4:5, :] = jnp.concatenate([right[0:1], left[1:2]], axis=1)
+    turn = 2.0 * comps[9]
+    comps[9] = jnp.cos(turn)
+    comps[10] = jnp.sin(turn)
+    turned = jnp.concatenate(
+        [group_fixed[t, block, 1] for t in range(8) for block in range(BLOCKS)]
+        + [jnp.zeros((HALF // 2, HALF), jnp.float32)],
+        axis=0,
+    ).T
+
+    def column(t, block, half):
+        at = 8 * t + 2 * block + half
+        return jnp.broadcast_to(turned[:, at : at + 1], (HALF, HALF))
+
+    nowhere = jnp.full((HALF, HALF), -1.0, jnp.float32)
+    low_rows = rows_of((HALF, HALF)) < BAND
+    for t in range(8):
+        for block in range(BLOCKS):
+            for half in range(2):
+                columns[6 * t + 1 + block, HALF * half : HALF * half + HALF, :] = column(
+                    t, block, half
+                )
+        columns[6 * t, 0:HALF, :] = nowhere
+        columns[6 * t, HALF:WIN, :] = jnp.where(low_rows, -1.0, column(max(t - 2, 0), BLOCKS - 1, 1))
+        columns[6 * t + 5, 0:HALF, :] = jnp.where(low_rows, column(min(t + 2, 7), 0, 0), -1.0)
+        columns[6 * t + 5, HALF:WIN, :] = nowhere
+
+    small.start_second()
+    big.start_second()
+    mid.start_second()
+    small.arrive()
+    over = make_lists(all_meta, group_meta, near_a, near_b, live_a, live_b, lag_a, lag_b)
+    copies = [
+        pltpu.make_async_copy(near_a, list_a, list_sems.at[0]),
+        pltpu.make_async_copy(near_b, list_b, list_sems.at[1]),
+    ]
+    for copy in copies:
+        copy.start()
+    into_a = placing(near_a[...], 6, 40)
+    into_b = placing(near_b[...], 0, 2 * BPD)
+    for copy in copies:
+        copy.wait()
+    big.arrive()
+    mid.arrive()
+
+    wide_lane = lanes((1, WIN)).astype(jnp.float32)
+
+    def doubled(row):
+        return jnp.concatenate([row, row], axis=1)
+
+    def nine(p, where_at, trig, live, lag):
+        turn = 2.0 * all_fixed[where_at + (0,)]
+        co2, si2 = jnp.cos(turn), jnp.sin(turn)
+        trig[p, 0:2, :] = co2
+        trig[p, 2:4, :] = si2
+        co, si = joined(co2), joined(si2)
+        f = joined(all_base[where_at])
+        weight = jnp.where(
+            wide_lane < doubled(live[pl.ds(p, 1), :]), doubled(lag[pl.ds(p, 1), :]), 0.0
+        )
+        return all_fixed[where_at + (1,)], [f, f * co, f * si] + weight_rows(weight, co, si)
+
+    def three(p, where_at, trig, source):
+        f = joined(source[where_at])
+        return [f, f * joined(trig[p, 0:2, :]), f * joined(trig[p, 2:4, :])]
+
+    def keep_rows(result, p, values):
+        for c, value in enumerate(values):
+            result[pl.ds(p, 1), WIN * c : WIN * c + WIN] = value
+
+    def gathered_rows(into, result, count):
+        return jnp.dot(
+            into, result[:, 0 : WIN * count], precision=HIGHEST, preferred_element_type=jnp.float32
+        )
+
+    def pair_first(p, carry):
+        code = list_a[p, 0]
+        places, values = nine(
+            p, locate(lax.shift_right_logical(code, 12)), trig_a, live_a, lag_a
+        )
+        picked = matches(columns[jnp.clip((code & 63) - 1, 0, 47)], places)
+        picked_a[p] = picked
+        keep_rows(result_a, p, split_product(values, picked))
+        return carry
+
+    lax.fori_loop(0, PAIRS, pair_first, 0, unroll=2)
+    out = gathered_rows(into_a, result_a, 9)
+    sums_out[...] = jnp.zeros_like(sums_out)
+    for t in range(8):
+        for c in range(9):
+            sums_out[t, 5 * c : 5 * c + 5, :] = out[5 * t : 5 * t + 5, WIN * c : WIN * c + WIN]
+    arriving = group.to_all(2, lambda t: sums_out.at[t], sums_in.at[me])
+    sums_in[me] = sums_out[me]
+    landed(arriving)
+    combined = sums_in[0]
+    for t in range(1, 8):
+        combined = combined + sums_in[t]
+    for c in range(9):
+        comps[c, 0:5, :] = combined[5 * c : 5 * c + 5]
+    m_aa, m_ab, m_ac, m_bb, m_bc, m_cc, det = adjugate(*(comps[c] for c in range(3, 9)))
+    co, si = comps[9], comps[10]
+    seg_row = rows_of((8, WIN))
+    at = lanes((8, WIN))
+    time = tm * SPAN + jnp.where(
+        seg_row < BLOCKS, seg_row * WIN + at, jnp.where(at < HALF, SPAN + at, at - WIN)
+    )
+    inside = (seg_row < BLOCKS) | ((seg_row == BLOCKS) & ((at < BAND) | (at >= WIN - BAND)))
+    live = (time >= 0) & (time < valid[0, 0]) & inside
+    scale = jnp.where(live, 1.0, 0.0) / det
+    factors[0] = (m_aa + m_ab * co + m_ac * si) * scale
+    factors[1] = (m_ab + m_bb * co + m_bc * si) * scale
+    factors[2] = (m_ac + m_bc * co + m_cc * si) * scale
+
+    def change():
+        return factors[0] * comps[0] + factors[1] * comps[1] + factors[2] * comps[2]
+
+    def filter_signal(signal, out):
+        halo_rows[0:1] = signal[4:5, HALF:]
+        for block in range(BLOCKS):
+            halo_rows[2 * block + 1 : 2 * block + 2] = signal[block : block + 1, :HALF]
+            halo_rows[2 * block + 2 : 2 * block + 3] = signal[block : block + 1, HALF:]
+        halo_rows[9:10] = signal[4:5, :HALF]
+        result = jnp.where(own_live, band_filter(halo_rows[...], band), 0.0)
+        for block in range(BLOCKS):
+            out[block] = result[2 * block : 2 * block + 2]
+        return result
+
+    signal_first = change()
+    filtered_first = filter_signal(signal_first, message)
+    own = halo_rows[1:9]
+    row_two[0] = (
+        jnp.where(lane == 0, total(base_own * own), 0.0)
+        + jnp.where(lane == 1, total(filtered_first * own), 0.0)
+        + jnp.where(lane == 2, over, 0.0)
+    )
+
+    pixel = rows_of((WIN, HALF)).astype(jnp.float32)
+
+    def owned_first(p, carry):
+        code = list_b[p, 0]
+        places, values = nine(
+            p, locate(lax.shift_right_logical(code, 6)), trig_b, live_b, lag_b
+        )
+        picked = matches(pixel, places)
+        picked_b[p] = picked
+        keep_rows(result_b, p, split_product(values, picked))
+        return carry
+
+    def owned_next(source):
+        def body(p, carry):
+            code = list_b[p, 0]
+            values = three(p, locate(lax.shift_right_logical(code, 6)), trig_b, source)
+            keep_rows(result_b, p, split_product(values, picked_b[p]))
+            return carry
+
+        return body
+
+    def owned_out(first, count, number):
+        out = gathered_rows(into_b, result_b, count)
+        for half in range(2):
+            for c in range(count):
+                own_part[half, first + c] = out[BPD * half : BPD * half + BPD, WIN * c : WIN * c + WIN]
+        span = pl.ds(first, count)
+        return group.to_partner(number, own_part.at[1 - core, span], partner_part.at[span])
+
+    def owned_along(first, count, number, arriving):
+        landed(arriving)
+        span = pl.ds(first, count)
+        x_part[x, span] = own_part[core, span] + partner_part[span]
+        return group.along(number, x_part.at[x, span])
+
+    def owned_sum(first, count):
+        span = pl.ds(first, count)
+        owned[span] = x_part[0, span] + x_part[1, span] + x_part[2, span] + x_part[3, span]
+
+    def sums_of(metas):
+        return jnp.sum(metas[...].reshape(32, 1, HALF), axis=0)
+
+    big, small = relays[1], smalls[1]
+    small.start_first()
+    big.start_first()
+    lax.fori_loop(0, SLOTS, owned_first, 0, unroll=2)
+    small.start_second()
+    big.start_second()
+    waiting_first = owned_out(0, 9, 5)
+    small.arrive()
+    sums = sums_of(meta_two)
+    big.arrive()
+
+    def pair_second(p, carry):
+        code = list_a[p, 0]
+        values = three(p, locate(lax.shift_right_logical(code, 12)), trig_a, all_first)
+        keep_rows(result_a, p, split_product(values, picked_a[p]))
+        return carry
+
+    lax.fori_loop(0, PAIRS, pair_second, 0, unroll=4)
+    out = gathered_rows(into_a, result_a, 3)
+    for t in range(8):
+        for c in range(3):
+            next_out[t, 5 * c : 5 * c + 5, :] = out[5 * t : 5 * t + 5, WIN * c : WIN * c + WIN]
+        next_out[t, 15:16, :] = doubled(sums)
+    arriving = group.to_all(3, lambda t: next_out.at[t], next_in.at[me])
+    next_in[me] = next_out[me]
+    landed(arriving)
+    combined = next_in[0]
+    for t in range(1, 8):
+        combined = combined + next_in[t]
+    for c in range(3):
+        comps[c, 0:5, :] = combined[5 * c : 5 * c + 5]
+    sums = combined[15:16, :HALF]
+    product, curve = sums[:, 0:1], sums[:, 1:2]
+    over_out[...] = jnp.broadcast_to(sums[:, 2:3], (1, HALF))
+    alpha = product / curve
+    filtered_second = filter_signal(signal_first - alpha * change(), message_two)
+    own = halo_rows[1:9]
+    row_two[1] = (
+        jnp.where(lane == 0, total((base_own - alpha * filtered_first) * own), 0.0)
+        + jnp.where(lane == 1, total(filtered_second * own), 0.0)
+        + jnp.where(lane == 2, total(filtered_first * own), 0.0)
+    )
+
+    big, small = relays[2], smalls[2]
+    small.start_first()
+    big.start_first()
+    first_along = owned_along(0, 9, 6, waiting_first)
+    lax.fori_loop(0, SLOTS, owned_next(all_first), 0, unroll=4)
+    waiting_second = owned_out(9, 3, 7)
+    small.start_second()
+    big.start_second()
+    second_along = owned_along(9, 3, 8, waiting_second)
+    small.arrive()
+    last_row[...] = sums_of(meta_three)
+    rows_in = group.to_all(4, lambda t: last_row, group_row.at[me])
+    group_row[me] = last_row[...]
+    big.arrive()
+    lax.fori_loop(0, SLOTS, owned_next(all_second), 0, unroll=4)
+    waiting_third = owned_out(12, 3, 9)
+    third_along = owned_along(12, 3, 10, waiting_third)
+
+    landed(rows_in)
+    sums = group_row[0]
+    for t in range(1, 8):
+        sums = sums + group_row[t]
+    product_next = sums[:, 0:1]
+    beta = product_next / product
+    curve_next = sums[:, 1:2] + 2.0 * beta * sums[:, 2:3] + beta * beta * curve
+    alpha_next = product_next / curve_next
+
+    def solve(r1, r2, r3):
+        i_aa, i_ab, i_ac, i_bb, i_bc, i_cc = (inverse[c] for c in range(6))
+        return (
+            i_aa * r1 + i_ab * r2 + i_ac * r3,
+            i_ab * r1 + i_bb * r2 + i_bc * r3,
+            i_ac * r1 + i_bc * r2 + i_cc * r3,
+        )
+
+    landed(first_along)
+    owned_sum(0, 9)
+    *minors, det = adjugate(*(owned[c] for c in range(3, 9)))
+    scale = 1.0 / det
+    for c, minor in enumerate(minors):
+        inverse[c] = minor * scale
+    landed(second_along)
+    owned_sum(9, 3)
+    start = solve(*(owned[c] for c in range(3)))
+    for c in range(3):
+        owned[c] = owned[c] - alpha * owned[9 + c]
+    middle = solve(*(owned[c] for c in range(3)))
+    for c in range(3):
+        solution_out[c] = alpha * start[c] + alpha_next * (middle[c] + beta * start[c])
+        owned[c] = owned[c] - alpha_next * beta * owned[9 + c]
+    landed(third_along)
+    owned_sum(12, 3)
+    final = solve(*(owned[c] - alpha_next * owned[12 + c] for c in range(3)))
+    for c in range(3):
+        residual_out[c] = final[c]
+    for mover in smalls + relays + [group]:
+        mover.finish()
+    for copy in halos:
+        copy.wait_send()
+
+
 def f32(*shape):
     return jax.ShapeDtypeStruct(shape, jnp.float32)
 
@@ -539,7 +1152,7 @@
     return rows.reshape(LABELS, 2, HALF), parts.reshape(DEVICES, HALF)
 
 
-def per_device(
+def any_lengths(
     time_streams, pol_angle, offsets, block_slots, hit_ids, valid_counts, filter_taps, white_weight
 ):
     valid = valid_counts.reshape(1)
@@ -615,6 +1228,61 @@
         scratch_shapes=[pltpu.VMEM((15, BPD, WIN), jnp.float32)],
         name="last",
     )(heads, nexts, lives, lag_zero, gathered, second, third, parts_two, parts_three)
+    return tuple(answers)
+
+
+def wide_buffer(*shape):
+    return pltpu.VMEM((8, 4) + shape, jnp.float32)
+
+
+def room(*shape):
+    return pltpu.VMEM(shape, jnp.float32)
+
+
+def per_device(*args):
+    (
+        time_streams, pol_angle, offsets, block_slots, hit_ids, valid_counts, filter_taps,
+        white_weight,
+    ) = args
+    fast = pl.pallas_call(
+        whole_kernel,
+        out_shape=(f32(3, BPD, WIN), f32(3, BPD, WIN), f32(1, HALF)),
+        in_specs=[smem] * 4 + [vmem] * 4,
+        out_specs=(vmem,) * 3,
+        scratch_shapes=[
+            room(2, 1, HALF), room(1, WIN), room(BLOCKS, 2, 2, HALF), room(1, HALF),
+            room(BLOCKS, 2, HALF), room(BLOCKS, 2, HALF), room(2, 1, HALF), room(BLOCKS, 2, HALF),
+            wide_buffer(BLOCKS, 2, 2, HALF), wide_buffer(BLOCKS, 2, HALF), wide_buffer(1, HALF),
+            wide_buffer(BLOCKS, 2, HALF), wide_buffer(1, HALF), wide_buffer(BLOCKS, 2, HALF),
+            wide_buffer(1, HALF),
+            room(8, BLOCKS, 2, 2, HALF), room(8, 1, HALF), room(8, 48, WIN), room(8, 48, WIN),
+            room(8, 16, WIN), room(8, 16, WIN), room(1, HALF), room(8, 1, HALF),
+            room(48, WIN, HALF),
+            pltpu.VMEM((PAIRS, WIN, WIN), jnp.bfloat16),
+            pltpu.VMEM((SLOTS, WIN, WIN), jnp.bfloat16),
+            room(PAIRS, 4, HALF), room(SLOTS, 4, HALF),
+            pltpu.SMEM((32, HALF), jnp.int32), pltpu.SMEM((24, HALF), jnp.int32),
+            room(32, HALF), room(24, HALF), room(32, HALF), room(24, HALF),
+            pltpu.VMEM((32, HALF), jnp.int32), pltpu.VMEM((24, HALF), jnp.int32),
+            room(32, 9 * WIN), room(24, 9 * WIN),
+            room(11, 8, WIN), room(3, 8, WIN), room(16, HALF),
+            room(2, 15, BPD, WIN), room(15, BPD, WIN), room(4, 15, BPD, WIN), room(15, BPD, WIN),
+            room(6, BPD, WIN),
+            pltpu.SemaphoreType.DMA((7, 10)), pltpu.SemaphoreType.DMA((7, 10)),
+            pltpu.SemaphoreType.DMA((7,)), pltpu.SemaphoreType.DMA((11, 8)),
+            pltpu.SemaphoreType.DMA((11, 8)), pltpu.SemaphoreType.DMA((2,)),
+            pltpu.SemaphoreType.DMA((2,)), pltpu.SemaphoreType.DMA((2,)),
+        ],
+        compiler_params=pltpu.CompilerParams(collective_id=3, has_side_effects=True),
+        name="whole",
+    )(
+        valid_counts, block_slots.reshape(1, BLOCKS), hit_ids, white_weight,
+        filter_taps.reshape(1, BAND + 1), time_streams.reshape(8, HALF),
+        pol_angle.reshape(8, HALF), offsets.reshape(8, HALF),
+    )
+    answers = lax.cond(
+        fast[2][0, 0] > 0.0, lambda f, *a: any_lengths(*a), lambda f, *a: f, fast[:2], *args
+    )
     return tuple(jnp.transpose(answer, (1, 0, 2)) for answer in answers)
 
 

time: 121 us -> 71.2 us (0.59)
  Pallas kernels: 110 us -> 67.3 us
  other arithmetic: 6.33 us -> 0 us
  local copies, waits for them, and re-layouts: 2.45 us -> 1.24 us
    pallas_call x6 -> x1, Pallas kernels: 110 us -> 67.3 us  [per_device(): pl.pallas_call(whole_kernel, out_shape=(f32(3, BPD, WIN), f32(3, BPD, WIN...]
    reduce_sum x1 -> x0, other arithmetic: 3.85 us -> none  [per_device(): counts = jnp.sum(same, axis=1, dtype=jnp.int32)]
where the time goes in v4:
time: 71.2 us; the launch traced here: 71.1 us
  Pallas kernels  67.3 us (95%)
  between operations  2.5 us (4%)
  local copies, waits for them, and re-layouts  1.24 us (2%)
    pallas_call x1, Pallas kernels, per_device(): pl.pallas_call(whole_kernel, out_shape=(f32(3, BPD, WIN), f32(3, BPD, WIN...  67.3 us

profile of v4, /device:TPU:1, one launch (start us, length us, event | category | flops | bytes accessed | tf_op | source)
XLA Modules:
  0.0 71.1 jit_solution(10847131019643494735)
XLA Ops:
  1.9 67.3 %whole.1 = (f32[3,16,256]{2,1,0:T(8,128)S(1)}, f32[3,16,256]{2,1,0:T(8,128)S(1)}, f32[1,128]{1,0:T(1,128)}) custom-call(s32[1,1]{1,0:T(1,128)S(6)} %copy.19.valid, s32[1,4]{1,0:T(1,128)} %bitcast.45, s32[1,128]{1,0:T(1,128)} %hits.1, f32[1,1]{1,0:T(1,128)S(6)} %copy.20.white, f32[1,65]{1,0:T(1,128)} %bitcast.48, f32[8,128]{1,0:T(8,128)} %bitcast.37, ...), custom_call_target="tpu_custom_call" | custom-call | tf_op jit(solution)/shard_map/whole/pallas_call | solution.py:1247
  69.8 0.6 copy.21
  70.5 0.6 copy.22
  (1 shorter events, 0.0 us)

commit v5 on v4

--- a/solution.py
+++ b/solution.py
@@ -14,7 +14,8 @@
 SPAN = 1024
 BLOCKS = 4
 DEVICES = 256
-PAIRS = 28
+PAIRS = 24
+TARGETS = 32
 SLOTS = 20
 LABELS = DEVICES * BLOCKS
 
@@ -681,13 +682,9 @@
     lives = lane_row([table[4 + j : 5 + j] for j in range(4)])
     lags = lane_row([table[8:9]] * 4)
     label = lanes((1, HALF)).astype(jnp.float32)
-    none = jnp.full((1, 1), -5.0, jnp.float32)
-    wanted = []
-    for t in range(8):
-        wanted.append(group_meta[t - 2][:, 3:4] if t >= 2 else none)
-        wanted += [group_meta[t][:, j : j + 1] for j in range(BLOCKS)]
-        wanted.append(group_meta[t + 2][:, 0:1] if t < 6 else none)
-    wanted = jnp.concatenate(wanted, axis=0)
+    wanted = jnp.concatenate(
+        [group_meta[t][:, j : j + 1] for t in range(8) for j in range(BLOCKS)], axis=0
+    )
     base = ((z * 4 + y) * 2 * BPD).astype(jnp.float32)
     mask = jnp.concatenate(
         [
@@ -699,15 +696,13 @@
     )
     ahead = jnp.where(rows_of((HALF, HALF)) < lanes((HALF, HALF)), 1.0, 0.0)
     within = jnp.dot(mask, ahead, precision=HIGHEST, preferred_element_type=jnp.float32)
-    totals = jnp.broadcast_to(jnp.sum(mask, axis=1, keepdims=True), (64, HALF))
-    above = jnp.where(
-        (rows_of((64, 64)) > lanes((64, 64))) & ((rows_of((64, 64)) >= 48) == (lanes((64, 64)) >= 48)),
-        1.0, 0.0,
-    )
+    totals = jnp.broadcast_to(jnp.sum(mask, axis=1, keepdims=True), (48, HALF))
+    row, col = rows_of((48, 48)), lanes((48, 48))
+    above = jnp.where((row > col) & (row < TARGETS), 1.0, 0.0)
     rank = within + jnp.dot(above, totals, precision=HIGHEST, preferred_element_type=jnp.float32)
     rank = jnp.where(mask > 0.0, rank, -1.0)
-    count_a = jnp.sum(totals[0:48, 0:1], axis=0, keepdims=True)
-    count_b = totals[48:49, 0:1]
+    count_a = jnp.sum(totals[0:TARGETS, 0:1], axis=0, keepdims=True)
+    count_b = totals[TARGETS : TARGETS + 1, 0:1]
     over = jnp.where((count_a > PAIRS) | (count_b > SLOTS), 1.0, 0.0)
 
     def spread(values):
@@ -720,18 +715,17 @@
 
     slot = rows_of((32, HALF)).astype(jnp.float32)
     code = jnp.zeros((32, HALF), jnp.float32)
-    for r in range(48):
-        row = 5 * (r // 6) + (4, 0, 1, 2, 3, 4)[r % 6]
-        code += jnp.where(slot == rank[r : r + 1], label * 4096.0 + ((row + 1) * 64.0 + r + 1.0), 0.0)
+    for r in range(TARGETS):
+        code += jnp.where(slot == rank[r : r + 1], label * 64.0 + (r + 1.0), 0.0)
     store(code, list_a, live_a, lag_a)
     slot = rows_of((24, HALF)).astype(jnp.float32)
-    code = jnp.where(slot == rank[48:49], label * 64.0 + (blocks - base + 1.0), 0.0)
+    code = jnp.where(slot == rank[TARGETS : TARGETS + 1], label * 64.0 + (blocks - base + 1.0), 0.0)
     store(code, list_b, live_b, lag_b)
     return over
 
 
-def placing(codes, shift, count):
-    row = (lax.shift_right_logical(codes, shift) & 63) - 1
+def placing(codes, count):
+    row = (codes & 63) - 1
     here = jnp.where(row == lanes(codes.shape), 1.0, 0.0)
     size = codes.shape[0]
     square = jnp.concatenate([here, jnp.zeros((HALF - size, HALF), jnp.float32)], axis=0).T
@@ -841,6 +835,7 @@
 
     comps[...] = jnp.zeros_like(comps)
     halo_rows[...] = jnp.zeros_like(halo_rows)
+    sums_out[...] = jnp.zeros_like(sums_out)
     result_a[...] = jnp.zeros_like(result_a)
     result_b[...] = jnp.zeros_like(result_b)
     landed(places_in)
@@ -863,18 +858,12 @@
         at = 8 * t + 2 * block + half
         return jnp.broadcast_to(turned[:, at : at + 1], (HALF, HALF))
 
-    nowhere = jnp.full((HALF, HALF), -1.0, jnp.float32)
-    low_rows = rows_of((HALF, HALF)) < BAND
     for t in range(8):
         for block in range(BLOCKS):
             for half in range(2):
-                columns[6 * t + 1 + block, HALF * half : HALF * half + HALF, :] = column(
+                columns[BLOCKS * t + block, HALF * half : HALF * half + HALF, :] = column(
                     t, block, half
                 )
-        columns[6 * t, 0:HALF, :] = nowhere
-        columns[6 * t, HALF:WIN, :] = jnp.where(low_rows, -1.0, column(max(t - 2, 0), BLOCKS - 1, 1))
-        columns[6 * t + 5, 0:HALF, :] = jnp.where(low_rows, column(min(t + 2, 7), 0, 0), -1.0)
-        columns[6 * t + 5, HALF:WIN, :] = nowhere
 
     small.start_second()
     big.start_second()
@@ -887,8 +876,8 @@
     ]
     for copy in copies:
         copy.start()
-    into_a = placing(near_a[...], 6, 40)
-    into_b = placing(near_b[...], 0, 2 * BPD)
+    into_a = placing(near_a[...], TARGETS)
+    into_b = placing(near_b[...], 2 * BPD)
     for copy in copies:
         copy.wait()
     big.arrive()
@@ -927,19 +916,27 @@
     def pair_first(p, carry):
         code = list_a[p, 0]
         places, values = nine(
-            p, locate(lax.shift_right_logical(code, 12)), trig_a, live_a, lag_a
-        )
-        picked = matches(columns[jnp.clip((code & 63) - 1, 0, 47)], places)
+            p, locate(lax.shift_right_logical(code, 6)), trig_a, live_a, lag_a
+        )
+        picked = matches(columns[jnp.clip((code & 63) - 1, 0, TARGETS - 1)], places)
         picked_a[p] = picked
         keep_rows(result_a, p, split_product(values, picked))
         return carry
 
     lax.fori_loop(0, PAIRS, pair_first, 0, unroll=2)
-    out = gathered_rows(into_a, result_a, 9)
-    sums_out[...] = jnp.zeros_like(sums_out)
-    for t in range(8):
-        for c in range(9):
-            sums_out[t, 5 * c : 5 * c + 5, :] = out[5 * t : 5 * t + 5, WIN * c : WIN * c + WIN]
+    def hand_out(count, target):
+        out = gathered_rows(into_a, result_a, count)
+        empty = jnp.zeros((1, HALF), jnp.float32)
+        for t in range(8):
+            for c in range(count):
+                at = WIN * c
+                first = BLOCKS * t
+                target[t, 5 * c : 5 * c + 4, :] = out[first : first + 4, at : at + WIN]
+                right = out[first + 8 : first + 9, at : at + HALF] if t < 6 else empty
+                left = out[first - 5 : first - 4, at + HALF : at + WIN] if t >= 2 else empty
+                target[t, 5 * c + 4 : 5 * c + 5, :] = jnp.concatenate([right, left], axis=1)
+
+    hand_out(9, sums_out)
     arriving = group.to_all(2, lambda t: sums_out.at[t], sums_in.at[me])
     sums_in[me] = sums_out[me]
     landed(arriving)
@@ -1040,15 +1037,13 @@
 
     def pair_second(p, carry):
         code = list_a[p, 0]
-        values = three(p, locate(lax.shift_right_logical(code, 12)), trig_a, all_first)
+        values = three(p, locate(lax.shift_right_logical(code, 6)), trig_a, all_first)
         keep_rows(result_a, p, split_product(values, picked_a[p]))
         return carry
 
     lax.fori_loop(0, PAIRS, pair_second, 0, unroll=4)
-    out = gathered_rows(into_a, result_a, 3)
+    hand_out(3, next_out)
     for t in range(8):
-        for c in range(3):
-            next_out[t, 5 * c : 5 * c + 5, :] = out[5 * t : 5 * t + 5, WIN * c : WIN * c + WIN]
         next_out[t, 15:16, :] = doubled(sums)
     arriving = group.to_all(3, lambda t: next_out.at[t], next_in.at[me])
     next_in[me] = next_out[me]
@@ -1257,7 +1252,7 @@
             wide_buffer(1, HALF),
             room(8, BLOCKS, 2, 2, HALF), room(8, 1, HALF), room(8, 48, WIN), room(8, 48, WIN),
             room(8, 16, WIN), room(8, 16, WIN), room(1, HALF), room(8, 1, HALF),
-            room(48, WIN, HALF),
+            room(TARGETS, WIN, HALF),
             pltpu.VMEM((PAIRS, WIN, WIN), jnp.bfloat16),
             pltpu.VMEM((SLOTS, WIN, WIN), jnp.bfloat16),
             room(PAIRS, 4, HALF), room(SLOTS, 4, HALF),

time: 71.2 us -> 70.2 us (0.986)
  Pallas kernels: 67.3 us -> 66.3 us
    pallas_call x1, Pallas kernels: 67.3 us -> 66.3 us  [per_device(): pl.pallas_call(whole_kernel, out_shape=(f32(3, BPD, WIN), f32(3, BPD, WIN...]
where the time goes in v5:
time: 70.2 us; the launch traced here: 70.1 us
  Pallas kernels  66.3 us (94%)
  between operations  2.5 us (4%)
  local copies, waits for them, and re-layouts  1.24 us (2%)
    pallas_call x1, Pallas kernels, per_device(): pl.pallas_call(whole_kernel, out_shape=(f32(3, BPD, WIN), f32(3, BPD, WIN...  66.3 us

profile of v5, /device:TPU:1, one launch (start us, length us, event | category | flops | bytes accessed | tf_op | source)
XLA Modules:
  0.0 70.1 jit_solution(17941743010707034660)
XLA Ops:
  1.9 66.3 %whole.1 = (f32[3,16,256]{2,1,0:T(8,128)S(1)}, f32[3,16,256]{2,1,0:T(8,128)S(1)}, f32[1,128]{1,0:T(1,128)}) custom-call(s32[1,1]{1,0:T(1,128)S(6)} %copy.19.valid, s32[1,4]{1,0:T(1,128)} %bitcast.45, s32[1,128]{1,0:T(1,128)} %hits.1, f32[1,1]{1,0:T(1,128)S(6)} %copy.20.white, f32[1,65]{1,0:T(1,128)} %bitcast.48, f32[8,128]{1,0:T(8,128)} %bitcast.37, ...), custom_call_target="tpu_custom_call" | custom-call | tf_op jit(solution)/shard_map/whole/pallas_call | solution.py:1242
  68.8 0.6 copy.21
  69.5 0.6 copy.22
  (1 shorter events, 0.0 us)

commit v6 on v5

--- a/solution.py
+++ b/solution.py
@@ -16,6 +16,7 @@
 DEVICES = 256
 PAIRS = 24
 TARGETS = 32
+UNROLL = 4
 SLOTS = 20
 LABELS = DEVICES * BLOCKS
 
@@ -737,7 +738,7 @@
     solution_out, residual_out, over_out,
     hold, taps_row, fixed, meta, base, message, row_two, message_two,
     all_fixed, all_base, all_meta, all_first, meta_two, all_second, meta_three,
-    group_fixed, group_meta, sums_out, sums_in, next_out, next_in, last_row, group_row,
+    group_fixed, group_meta, sums_out, sums_in, base_out, base_in, next_out, next_in, last_row, group_row,
     columns, picked_a, picked_b, trig_a, trig_b, list_a, list_b, live_a, live_b, lag_a, lag_b,
     near_a, near_b, result_a, result_b, comps, factors, halo_rows,
     own_part, partner_part, x_part, owned, inverse,
@@ -836,6 +837,7 @@
     comps[...] = jnp.zeros_like(comps)
     halo_rows[...] = jnp.zeros_like(halo_rows)
     sums_out[...] = jnp.zeros_like(sums_out)
+    base_out[...] = jnp.zeros_like(base_out)
     result_a[...] = jnp.zeros_like(result_a)
     result_b[...] = jnp.zeros_like(result_b)
     landed(places_in)
@@ -867,7 +869,6 @@
 
     small.start_second()
     big.start_second()
-    mid.start_second()
     small.arrive()
     over = make_lists(all_meta, group_meta, near_a, near_b, live_a, live_b, lag_a, lag_b)
     copies = [
@@ -876,29 +877,28 @@
     ]
     for copy in copies:
         copy.start()
+    mid.start_second()
     into_a = placing(near_a[...], TARGETS)
     into_b = placing(near_b[...], 2 * BPD)
     for copy in copies:
         copy.wait()
     big.arrive()
-    mid.arrive()
 
     wide_lane = lanes((1, WIN)).astype(jnp.float32)
 
     def doubled(row):
         return jnp.concatenate([row, row], axis=1)
 
-    def nine(p, where_at, trig, live, lag):
+    def six(p, where_at, trig, live, lag):
         turn = 2.0 * all_fixed[where_at + (0,)]
         co2, si2 = jnp.cos(turn), jnp.sin(turn)
         trig[p, 0:2, :] = co2
         trig[p, 2:4, :] = si2
         co, si = joined(co2), joined(si2)
-        f = joined(all_base[where_at])
         weight = jnp.where(
             wide_lane < doubled(live[pl.ds(p, 1), :]), doubled(lag[pl.ds(p, 1), :]), 0.0
         )
-        return all_fixed[where_at + (1,)], [f, f * co, f * si] + weight_rows(weight, co, si)
+        return all_fixed[where_at + (1,)], co, si, weight_rows(weight, co, si)
 
     def three(p, where_at, trig, source):
         f = joined(source[where_at])
@@ -913,9 +913,9 @@
             into, result[:, 0 : WIN * count], precision=HIGHEST, preferred_element_type=jnp.float32
         )
 
-    def pair_first(p, carry):
+    def pair_weights(p, carry):
         code = list_a[p, 0]
-        places, values = nine(
+        places, _, _, values = six(
             p, locate(lax.shift_right_logical(code, 6)), trig_a, live_a, lag_a
         )
         picked = matches(columns[jnp.clip((code & 63) - 1, 0, TARGETS - 1)], places)
@@ -923,7 +923,17 @@
         keep_rows(result_a, p, split_product(values, picked))
         return carry
 
-    lax.fori_loop(0, PAIRS, pair_first, 0, unroll=2)
+    def pair_next(source):
+        def body(p, carry):
+            code = list_a[p, 0]
+            values = three(p, locate(lax.shift_right_logical(code, 6)), trig_a, source)
+            keep_rows(result_a, p, split_product(values, picked_a[p]))
+            return carry
+
+        return body
+
+    lax.fori_loop(0, PAIRS, pair_weights, 0, unroll=UNROLL)
+
     def hand_out(count, target):
         out = gathered_rows(into_a, result_a, count)
         empty = jnp.zeros((1, HALF), jnp.float32)
@@ -936,15 +946,24 @@
                 left = out[first - 5 : first - 4, at + HALF : at + WIN] if t >= 2 else empty
                 target[t, 5 * c + 4 : 5 * c + 5, :] = jnp.concatenate([right, left], axis=1)
 
-    hand_out(9, sums_out)
+    def sum_of(arrived):
+        combined = arrived[0]
+        for t in range(1, 8):
+            combined = combined + arrived[t]
+        return combined
+
+    hand_out(6, sums_out)
     arriving = group.to_all(2, lambda t: sums_out.at[t], sums_in.at[me])
     sums_in[me] = sums_out[me]
+    mid.arrive()
+    lax.fori_loop(0, PAIRS, pair_next(all_base), 0, unroll=4)
+    hand_out(3, base_out)
+    arriving_base = group.to_all(11, lambda t: base_out.at[t], base_in.at[me])
+    base_in[me] = base_out[me]
     landed(arriving)
-    combined = sums_in[0]
-    for t in range(1, 8):
-        combined = combined + sums_in[t]
-    for c in range(9):
-        comps[c, 0:5, :] = combined[5 * c : 5 * c + 5]
+    combined = sum_of(sums_in)
+    for c in range(6):
+        comps[3 + c, 0:5, :] = combined[5 * c : 5 * c + 5]
     m_aa, m_ab, m_ac, m_bb, m_bc, m_cc, det = adjugate(*(comps[c] for c in range(3, 9)))
     co, si = comps[9], comps[10]
     seg_row = rows_of((8, WIN))
@@ -958,6 +977,10 @@
     factors[0] = (m_aa + m_ab * co + m_ac * si) * scale
     factors[1] = (m_ab + m_bb * co + m_bc * si) * scale
     factors[2] = (m_ac + m_bc * co + m_cc * si) * scale
+    landed(arriving_base)
+    combined = sum_of(base_in)
+    for c in range(3):
+        comps[c, 0:5, :] = combined[5 * c : 5 * c + 5]
 
     def change():
         return factors[0] * comps[0] + factors[1] * comps[1] + factors[2] * comps[2]
@@ -986,9 +1009,10 @@
 
     def owned_first(p, carry):
         code = list_b[p, 0]
-        places, values = nine(
-            p, locate(lax.shift_right_logical(code, 6)), trig_b, live_b, lag_b
-        )
+        where_at = locate(lax.shift_right_logical(code, 6))
+        places, co, si, values = six(p, where_at, trig_b, live_b, lag_b)
+        f = joined(all_base[where_at])
+        values = [f, f * co, f * si] + values
         picked = matches(pixel, places)
         picked_b[p] = picked
         keep_rows(result_b, p, split_product(values, picked))
@@ -1035,22 +1059,14 @@
     sums = sums_of(meta_two)
     big.arrive()
 
-    def pair_second(p, carry):
-        code = list_a[p, 0]
-        values = three(p, locate(lax.shift_right_logical(code, 6)), trig_a, all_first)
-        keep_rows(result_a, p, split_product(values, picked_a[p]))
-        return carry
-
-    lax.fori_loop(0, PAIRS, pair_second, 0, unroll=4)
+    lax.fori_loop(0, PAIRS, pair_next(all_first), 0, unroll=4)
     hand_out(3, next_out)
     for t in range(8):
         next_out[t, 15:16, :] = doubled(sums)
     arriving = group.to_all(3, lambda t: next_out.at[t], next_in.at[me])
     next_in[me] = next_out[me]
     landed(arriving)
-    combined = next_in[0]
-    for t in range(1, 8):
-        combined = combined + next_in[t]
+    combined = sum_of(next_in)
     for c in range(3):
         comps[c, 0:5, :] = combined[5 * c : 5 * c + 5]
     sums = combined[15:16, :HALF]
@@ -1250,7 +1266,8 @@
             wide_buffer(BLOCKS, 2, 2, HALF), wide_buffer(BLOCKS, 2, HALF), wide_buffer(1, HALF),
             wide_buffer(BLOCKS, 2, HALF), wide_buffer(1, HALF), wide_buffer(BLOCKS, 2, HALF),
             wide_buffer(1, HALF),
-            room(8, BLOCKS, 2, 2, HALF), room(8, 1, HALF), room(8, 48, WIN), room(8, 48, WIN),
+            room(8, BLOCKS, 2, 2, HALF), room(8, 1, HALF), room(8, 32, WIN), room(8, 32, WIN),
+            room(8, 16, WIN), room(8, 16, WIN),
             room(8, 16, WIN), room(8, 16, WIN), room(1, HALF), room(8, 1, HALF),
             room(TARGETS, WIN, HALF),
             pltpu.VMEM((PAIRS, WIN, WIN), jnp.bfloat16),
@@ -1264,8 +1281,8 @@
             room(2, 15, BPD, WIN), room(15, BPD, WIN), room(4, 15, BPD, WIN), room(15, BPD, WIN),
             room(6, BPD, WIN),
             pltpu.SemaphoreType.DMA((7, 10)), pltpu.SemaphoreType.DMA((7, 10)),
-            pltpu.SemaphoreType.DMA((7,)), pltpu.SemaphoreType.DMA((11, 8)),
-            pltpu.SemaphoreType.DMA((11, 8)), pltpu.SemaphoreType.DMA((2,)),
+            pltpu.SemaphoreType.DMA((7,)), pltpu.SemaphoreType.DMA((12, 8)),
+            pltpu.SemaphoreType.DMA((12, 8)), pltpu.SemaphoreType.DMA((2,)),
             pltpu.SemaphoreType.DMA((2,)), pltpu.SemaphoreType.DMA((2,)),
         ],
         compiler_params=pltpu.CompilerParams(collective_id=3, has_side_effects=True),

time: 70.2 us -> 68.4 us (0.974)
  Pallas kernels: 66.3 us -> 64.5 us
    pallas_call x1, Pallas kernels: 66.3 us -> 64.5 us  [per_device(): pl.pallas_call(whole_kernel, out_shape=(f32(3, BPD, WIN), f32(3, BPD, WIN...]
where the time goes in v6:
time: 68.4 us; the launch traced here: 68.2 us
  Pallas kernels  64.5 us (94%)
  between operations  2.5 us (4%)
  local copies, waits for them, and re-layouts  1.24 us (2%)
    pallas_call x1, Pallas kernels, per_device(): pl.pallas_call(whole_kernel, out_shape=(f32(3, BPD, WIN), f32(3, BPD, WIN...  64.5 us

profile of v6, /device:TPU:1, one launch (start us, length us, event | category | flops | bytes accessed | tf_op | source)
XLA Modules:
  0.0 68.2 jit_solution(8318145676867304566)
XLA Ops:
  1.9 64.5 %whole.1 = (f32[3,16,256]{2,1,0:T(8,128)S(1)}, f32[3,16,256]{2,1,0:T(8,128)S(1)}, f32[1,128]{1,0:T(1,128)}) custom-call(s32[1,1]{1,0:T(1,128)S(6)} %copy.19.valid, s32[1,4]{1,0:T(1,128)} %bitcast.45, s32[1,128]{1,0:T(1,128)} %hits.1, f32[1,1]{1,0:T(1,128)S(6)} %copy.20.white, f32[1,65]{1,0:T(1,128)} %bitcast.48, f32[8,128]{1,0:T(8,128)} %bitcast.37, ...), custom_call_target="tpu_custom_call" | custom-call | tf_op jit(solution)/shard_map/whole/pallas_call | solution.py:1258
  67.0 0.6 copy.21
  67.6 0.6 copy.22
  (1 shorter events, 0.0 us)

commit v7 on v6

--- a/solution.py
+++ b/solution.py
@@ -719,7 +719,7 @@
     for r in range(TARGETS):
         code += jnp.where(slot == rank[r : r + 1], label * 64.0 + (r + 1.0), 0.0)
     store(code, list_a, live_a, lag_a)
-    slot = rows_of((24, HALF)).astype(jnp.float32)
+    slot = rows_of((32, HALF)).astype(jnp.float32)
     code = jnp.where(slot == rank[TARGETS : TARGETS + 1], label * 64.0 + (blocks - base + 1.0), 0.0)
     store(code, list_b, live_b, lag_b)
     return over
@@ -735,7 +735,7 @@
 
 def whole_kernel(
     valid, slots, hits, white, taps, stream, angle, offset,
-    solution_out, residual_out, over_out,
+    answers_out, over_out,
     hold, taps_row, fixed, meta, base, message, row_two, message_two,
     all_fixed, all_base, all_meta, all_first, meta_two, all_second, meta_three,
     group_fixed, group_meta, sums_out, sums_in, base_out, base_in, next_out, next_in, last_row, group_row,
@@ -880,6 +880,8 @@
     mid.start_second()
     into_a = placing(near_a[...], TARGETS)
     into_b = placing(near_b[...], 2 * BPD)
+    into_a = jnp.concatenate([into_a] * 3, axis=1).astype(jnp.bfloat16)
+    into_b = jnp.concatenate([into_b] * 3, axis=1).astype(jnp.bfloat16)
     for copy in copies:
         copy.wait()
     big.arrive()
@@ -909,9 +911,13 @@
             result[pl.ds(p, 1), WIN * c : WIN * c + WIN] = value
 
     def gathered_rows(into, result, count):
-        return jnp.dot(
-            into, result[:, 0 : WIN * count], precision=HIGHEST, preferred_element_type=jnp.float32
-        )
+        values = result[:, 0 : WIN * count]
+        high = values.astype(jnp.bfloat16)
+        rest = values - high.astype(jnp.float32)
+        middle = rest.astype(jnp.bfloat16)
+        low = (rest - middle.astype(jnp.float32)).astype(jnp.bfloat16)
+        parts = jnp.concatenate([high, middle, low], axis=0)
+        return jnp.dot(into, parts, preferred_element_type=jnp.float32)
 
     def pair_weights(p, carry):
         code = list_a[p, 0]
@@ -1129,13 +1135,13 @@
         owned[c] = owned[c] - alpha * owned[9 + c]
     middle = solve(*(owned[c] for c in range(3)))
     for c in range(3):
-        solution_out[c] = alpha * start[c] + alpha_next * (middle[c] + beta * start[c])
+        answers_out[c] = alpha * start[c] + alpha_next * (middle[c] + beta * start[c])
         owned[c] = owned[c] - alpha_next * beta * owned[9 + c]
     landed(third_along)
     owned_sum(12, 3)
     final = solve(*(owned[c] - alpha_next * owned[12 + c] for c in range(3)))
     for c in range(3):
-        residual_out[c] = final[c]
+        answers_out[3 + c] = final[c]
     for mover in smalls + relays + [group]:
         mover.finish()
     for copy in halos:
@@ -1257,9 +1263,9 @@
     ) = args
     fast = pl.pallas_call(
         whole_kernel,
-        out_shape=(f32(3, BPD, WIN), f32(3, BPD, WIN), f32(1, HALF)),
+        out_shape=(f32(6, BPD, WIN), f32(1, HALF)),
         in_specs=[smem] * 4 + [vmem] * 4,
-        out_specs=(vmem,) * 3,
+        out_specs=(vmem,) * 2,
         scratch_shapes=[
             room(2, 1, HALF), room(1, WIN), room(BLOCKS, 2, 2, HALF), room(1, HALF),
             room(BLOCKS, 2, HALF), room(BLOCKS, 2, HALF), room(2, 1, HALF), room(BLOCKS, 2, HALF),
@@ -1273,10 +1279,10 @@
             pltpu.VMEM((PAIRS, WIN, WIN), jnp.bfloat16),
             pltpu.VMEM((SLOTS, WIN, WIN), jnp.bfloat16),
             room(PAIRS, 4, HALF), room(SLOTS, 4, HALF),
-            pltpu.SMEM((32, HALF), jnp.int32), pltpu.SMEM((24, HALF), jnp.int32),
-            room(32, HALF), room(24, HALF), room(32, HALF), room(24, HALF),
-            pltpu.VMEM((32, HALF), jnp.int32), pltpu.VMEM((24, HALF), jnp.int32),
-            room(32, 9 * WIN), room(24, 9 * WIN),
+            pltpu.SMEM((32, HALF), jnp.int32), pltpu.SMEM((32, HALF), jnp.int32),
+            room(32, HALF), room(32, HALF), room(32, HALF), room(32, HALF),
+            pltpu.VMEM((32, HALF), jnp.int32), pltpu.VMEM((32, HALF), jnp.int32),
+            room(32, 9 * WIN), room(32, 9 * WIN),
             room(11, 8, WIN), room(3, 8, WIN), room(16, HALF),
             room(2, 15, BPD, WIN), room(15, BPD, WIN), room(4, 15, BPD, WIN), room(15, BPD, WIN),
             room(6, BPD, WIN),
@@ -1293,9 +1299,10 @@
         pol_angle.reshape(8, HALF), offsets.reshape(8, HALF),
     )
     answers = lax.cond(
-        fast[2][0, 0] > 0.0, lambda f, *a: any_lengths(*a), lambda f, *a: f, fast[:2], *args
-    )
-    return tuple(jnp.transpose(answer, (1, 0, 2)) for answer in answers)
+        fast[1][0, 0] > 0.0, lambda f, *a: jnp.concatenate(any_lengths(*a)), lambda f, *a: f,
+        fast[0], *args,
+    )
+    return tuple(jnp.transpose(part, (1, 0, 2)) for part in (answers[:3], answers[3:]))
 
 
 def solution(mesh):

time: 68.4 us -> 67.6 us (0.988)
    unnamed x2 -> x0, local copies, waits for them, and re-layouts: 1.24 us -> none
where the time goes in v7:
time: 67.6 us; the launch traced here: 67.4 us
  Pallas kernels  64.2 us (95%)
  between operations  2.57 us (4%)
    pallas_call x1, Pallas kernels, per_device(): pl.pallas_call(whole_kernel, out_shape=(f32(6, BPD, WIN), f32(1, HALF)),...  64.2 us

profile of v7, /device:TPU:1, one launch (start us, length us, event | category | flops | bytes accessed | tf_op | source)
XLA Modules:
  0.0 67.4 jit_solution(7419827198142195988)
XLA Ops:
  1.9 64.2 %whole.1 = (f32[6,16,256]{2,1,0:T(8,128)S(1)}, f32[1,128]{1,0:T(1,128)}) custom-call(s32[1,1]{1,0:T(1,128)S(6)} %copy.15.valid, s32[1,4]{1,0:T(1,128)} %bitcast.45, s32[1,128]{1,0:T(1,128)} %hits.1, f32[1,1]{1,0:T(1,128)S(6)} %copy.16.white, f32[1,65]{1,0:T(1,128)} %bitcast.48, f32[8,128]{1,0:T(8,128)} %bitcast.37, f32[8,128]{1,0:T(8,128)} %bitcast.39, ...), custom_call_target="tpu_custom_call" | custom-call | tf_op jit(solution)/shard_map/whole/pallas_call | solution.py:1264
  66.8 0.6 slice_bitcast_fusion
  (1 shorter events, 0.0 us)

commit v8 on v7

--- a/solution.py
+++ b/solution.py
@@ -962,7 +962,7 @@
     arriving = group.to_all(2, lambda t: sums_out.at[t], sums_in.at[me])
     sums_in[me] = sums_out[me]
     mid.arrive()
-    lax.fori_loop(0, PAIRS, pair_next(all_base), 0, unroll=4)
+    lax.fori_loop(0, PAIRS, pair_next(all_base), 0, unroll=12)
     hand_out(3, base_out)
     arriving_base = group.to_all(11, lambda t: base_out.at[t], base_in.at[me])
     base_in[me] = base_out[me]
@@ -1065,7 +1065,7 @@
     sums = sums_of(meta_two)
     big.arrive()
 
-    lax.fori_loop(0, PAIRS, pair_next(all_first), 0, unroll=4)
+    lax.fori_loop(0, PAIRS, pair_next(all_first), 0, unroll=12)
     hand_out(3, next_out)
     for t in range(8):
         next_out[t, 15:16, :] = doubled(sums)
@@ -1101,7 +1101,7 @@
     rows_in = group.to_all(4, lambda t: last_row, group_row.at[me])
     group_row[me] = last_row[...]
     big.arrive()
-    lax.fori_loop(0, SLOTS, owned_next(all_second), 0, unroll=4)
+    lax.fori_loop(0, SLOTS, owned_next(all_second), 0, unroll=10)
     waiting_third = owned_out(12, 3, 9)
     third_along = owned_along(12, 3, 10, waiting_third)
 

time: 67.6 us -> 66.5 us (0.984)
  Pallas kernels: 64.2 us -> 63.2 us
    pallas_call x1, Pallas kernels: 64.2 us -> 63.2 us  [per_device(): pl.pallas_call(whole_kernel, out_shape=(f32(6, BPD, WIN), f32(1, HALF)),...]
where the time goes in v8:
time: 66.5 us; the launch traced here: 66.4 us
  Pallas kernels  63.2 us (95%)
  between operations  2.57 us (4%)
    pallas_call x1, Pallas kernels, per_device(): pl.pallas_call(whole_kernel, out_shape=(f32(6, BPD, WIN), f32(1, HALF)),...  63.2 us

profile of v8, /device:TPU:1, one launch (start us, length us, event | category | flops | bytes accessed | tf_op | source)
XLA Modules:
  0.0 66.4 jit_solution(1590485126587699185)
XLA Ops:
  1.9 63.2 %whole.1 = (f32[6,16,256]{2,1,0:T(8,128)S(1)}, f32[1,128]{1,0:T(1,128)}) custom-call(s32[1,1]{1,0:T(1,128)S(6)} %copy.15.valid, s32[1,4]{1,0:T(1,128)} %bitcast.45, s32[1,128]{1,0:T(1,128)} %hits.1, f32[1,1]{1,0:T(1,128)S(6)} %copy.16.white, f32[1,65]{1,0:T(1,128)} %bitcast.48, f32[8,128]{1,0:T(8,128)} %bitcast.37, f32[8,128]{1,0:T(8,128)} %bitcast.39, ...), custom_call_target="tpu_custom_call" | custom-call | tf_op jit(solution)/shard_map/whole/pallas_call | solution.py:1264
  65.8 0.6 slice_bitcast_fusion
  (1 shorter events, 0.0 us)
